TPU v7x, 512 devices: a whole 4x8x8 slice. The times are simulated.
512 devices in a mesh: tm: 32 (over z_hi, y, core), space: 16 (over x, z_lo).
Axes of the slice: x: 4, y: 8, z: 8 (z_hi: 2, z_lo: 4; z = z_hi * 4 + z_lo), core: 2. Of those that a mesh axis runs over, the one named last changes fastest.
Arguments:
- state: float32 [1024, 384, 128], P('tm', 'space'), may hold values from -6 to 6
- forcing: float32 [1024, 384, 128], P('tm', 'space'), may hold values from -6 to 6
- initial: float32 [384, 128], P('space'), may hold values from -6 to 6
- blocks: bfloat16 [5, 384, 128, 128], P(None, 'space'), may hold values from -0.25 to 0.25
- precond: bfloat16 [384, 128, 128], P('space'), may hold values from -0.5 to 0.5
- couple: int32 [384, 5], P('space'), may hold values from -2 to 2
Outputs:
- corrected: float32 [1024, 384, 128], P('tm', 'space')
Inputs may be any that keep to these rules, and one draw needn't show every extreme that they name: Row j, slot s couples to block row j + couple[j, s].
All inputs are finite; a program needn't handle non-finite values.
Results may differ from a plain program's by a relative error of at most 0.002.
Values may be sent and summed in bfloat16 or wider, within the bound.
No kernel may reach another device: no remote copies, remote signals or barrier semaphores. Data moves between devices by JAX's collectives and lax.ppermute only.
A program may use at most 64 MiB of HBM per device.

v0:
```python
import math

import jax
import jax.numpy as jnp
from jax import lax
from jax.sharding import PartitionSpec as P

SWEEPS = 2


alpha_rate = 0.5
time_step = 0.5
relaxation = 0.7


def from_behind(block, axis, distance):
    devices = range(lax.axis_size(axis))
    route = [(i - distance, i) for i in devices if i - distance in devices]
    return lax.ppermute(block, axis, route)


def extended(block, sides, width):
    for axis, dim in sides:
        count = lax.axis_size(axis)
        forward = [(i, i + 1) for i in range(count - 1)]
        backward = [(target, source) for source, target in forward]
        low = lax.ppermute(
            lax.slice_in_dim(block, block.shape[dim] - width, None, axis=dim), axis, forward
        )
        high = lax.ppermute(lax.slice_in_dim(block, 0, width, axis=dim), axis, backward)
        block = jnp.concatenate([low, block, high], axis=dim)
    return block


def from_partner(block, axis, stride):
    count = lax.axis_size(axis)
    route = []
    for low in range(count):
        high = low | 1 << stride
        if high != low and high < count:
            route += [(low, high), (high, low)]
    return lax.ppermute(block, axis, route)


def apply_padded(padded, blocks, couple):
    width = padded.shape[1] - 4
    total = None
    for column in range(5):
        chosen = padded[:, 2 : 2 + width]
        for offset in range(-2, 3):
            picked = (couple[:, column] == offset)[None, :, None]
            chosen = jnp.where(picked, padded[:, 2 + offset : 2 + offset + width], chosen)
        term = jnp.einsum(
            "fbj,bij->fbi", chosen, blocks[column], preferred_element_type=jnp.float32
        )
        total = term if total is None else total + term
    return total


def on_device(state, forcing, initial, blocks, precond, couple):
    local_steps = state.shape[0]
    devices_tm = lax.axis_size("tm")
    position = lax.axis_index("tm")
    total_steps = local_steps * devices_tm
    level_count = devices_tm.bit_length() - 1
    highest = lax.Precision.HIGHEST
    last_step = from_behind(state[-1:], "tm", 1)
    first_prev = jnp.where(position == 0, initial[None], last_step)
    previous = jnp.concatenate([first_prev, state[:-1]], 0)
    squares = (0.5 * state * state).astype(jnp.bfloat16)
    padded = extended(squares, (("space", 1),), 2)
    flux = apply_padded(padded, blocks, couple)
    residual = forcing - state + previous - time_step * flux
    steps_global = position * local_steps + jnp.arange(local_steps, dtype=jnp.int32)
    log_rate = math.log(alpha_rate) / total_steps
    scaled = residual * jnp.exp(steps_global.astype(jnp.float32) * log_rate)[:, None, None]
    cur_re = scaled
    cur_im = jnp.zeros_like(scaled)
    for level in range(level_count):
        bit_number = level_count - 1 - level
        half = 1 << bit_number
        other = from_partner(jnp.stack([cur_re, cur_im]), "tm", bit_number)
        upper = position >> bit_number & 1 == 1
        angle = -2.0 * math.pi * (position % half).astype(jnp.float32) / (2 * half)
        tw_re = jnp.cos(angle)
        tw_im = jnp.sin(angle)
        diff_re = other[0] - cur_re
        diff_im = other[1] - cur_im
        new_re = jnp.where(upper, diff_re * tw_re - diff_im * tw_im, cur_re + other[0])
        new_im = jnp.where(upper, diff_re * tw_im + diff_im * tw_re, cur_im + other[1])
        cur_re, cur_im = (new_re, new_im)
    freq_base = jnp.zeros((), jnp.int32)
    for level in range(level_count):
        freq_base = freq_base + (position >> level & 1) * (1 << level_count - 1 - level)
    part_re, part_im = (cur_re, cur_im)
    local_index = jnp.arange(local_steps, dtype=jnp.int32)
    freq = freq_base + devices_tm * local_index
    product = freq[:, None] * local_index[None, :] % total_steps
    angle_table = 2.0 * math.pi * product.astype(jnp.float32) / total_steps
    table_re = jnp.cos(angle_table)
    table_im = -jnp.sin(angle_table)
    spec_re = jnp.einsum("qm,mbc->qbc", table_re, part_re, precision=highest) - jnp.einsum(
        "qm,mbc->qbc", table_im, part_im, precision=highest
    )
    spec_im = jnp.einsum("qm,mbc->qbc", table_re, part_im, precision=highest) + jnp.einsum(
        "qm,mbc->qbc", table_im, part_re, precision=highest
    )
    theta = 2.0 * math.pi * freq.astype(jnp.float32) / total_steps
    rate = math.exp(log_rate)
    lam_re = (1.0 - rate * jnp.cos(theta))[:, None, None]
    lam_im = (rate * jnp.sin(theta))[:, None, None]
    denom = (1.0 + lam_re) ** 2 + lam_im**2
    coef_re = (1.0 + lam_re) / denom
    coef_im = -lam_im / denom
    sol_re = None
    sol_im = None
    for sweep in range(SWEEPS):
        if sweep == 0:
            res_re, res_im = (spec_re, spec_im)
        else:
            stacked = jnp.concatenate([sol_re, sol_im], 0).astype(jnp.bfloat16)
            padded_sol = extended(stacked, (("space", 1),), 2)
            applied = apply_padded(padded_sol, blocks, couple)
            res_re = (
                spec_re - (lam_re * sol_re - lam_im * sol_im) - time_step * applied[:local_steps]
            )
            res_im = (
                spec_im - (lam_re * sol_im + lam_im * sol_re) - time_step * applied[local_steps:]
            )
        rounded = jnp.concatenate([res_re, res_im], 0).astype(jnp.bfloat16)
        gres = jnp.einsum("fbj,bij->fbi", rounded, precond, preferred_element_type=jnp.float32)
        g_re = gres[:local_steps]
        g_im = gres[local_steps:]
        step_re = relaxation * (coef_re * g_re - coef_im * g_im)
        step_im = relaxation * (coef_re * g_im + coef_im * g_re)
        if sweep == 0:
            sol_re, sol_im = (step_re, step_im)
        else:
            sol_re = sol_re + step_re
            sol_im = sol_im + step_im
    back_re = (
        jnp.einsum("qm,qbc->mbc", table_re, sol_re, precision=highest)
        + jnp.einsum("qm,qbc->mbc", table_im, sol_im, precision=highest)
    ) / local_steps
    back_im = (
        jnp.einsum("qm,qbc->mbc", table_re, sol_im, precision=highest)
        - jnp.einsum("qm,qbc->mbc", table_im, sol_re, precision=highest)
    ) / local_steps
    cur_re, cur_im = (back_re, back_im)
    for bit_number in range(level_count):
        half = 1 << bit_number
        other = from_partner(jnp.stack([cur_re, cur_im]), "tm", bit_number)
        upper = position >> bit_number & 1 == 1
        angle = -2.0 * math.pi * (position % half).astype(jnp.float32) / (2 * half)
        conj_re = jnp.cos(angle)
        conj_im = -jnp.sin(angle)
        other_tw_re = other[0] * conj_re - other[1] * conj_im
        other_tw_im = other[0] * conj_im + other[1] * conj_re
        mine_tw_re = cur_re * conj_re - cur_im * conj_im
        mine_tw_im = cur_re * conj_im + cur_im * conj_re
        new_re = jnp.where(upper, 0.5 * (other[0] - mine_tw_re), 0.5 * (cur_re + other_tw_re))
        new_im = jnp.where(upper, 0.5 * (other[1] - mine_tw_im), 0.5 * (cur_im + other_tw_im))
        cur_re, cur_im = (new_re, new_im)
    change = cur_re * jnp.exp(-steps_global.astype(jnp.float32) * log_rate)[:, None, None]
    return state + change


def solution(mesh):
    placed = (
        P("tm", "space", None),
        P("tm", "space", None),
        P("space", None),
        P(None, "space", None, None),
        P("space", None, None),
        P("space", None),
    )
    return jax.shard_map(
        on_device, mesh=mesh, in_specs=placed, out_specs=P("tm", "space", None), check_vma=False
    )
```

profile of v0, /device:TPU:27, one launch (start us, length us, event | category | flops | bytes accessed | tf_op | source)
XLA Modules:
  0.0 344.8 jit_solution(8418257847120855641)
XLA Ops:
  0.8 5.0 %collective-permute-start = (f32[1,24,128]{2,0,1:T(1,128)S(1)}, f32[1,24,128]{2,0,1:T(1,128)S(1)}, u32[]{:S(2)}, u32[]{:S(2)}) collective-permute-start(f32[1,24,128]{2,0,1:T(1,128)S(1)} %bitcast.328), channel_id=1, source_target_pairs={{0,16},{16,32},{32,48},{48,64},{64,80},{80,96},{96,112},{112,128},... | collective-permute-start | bytes 36872 | tf_op jit(solution)/shard_map/ppermute | solution.py:19
  5.8 1.1 fusion.25
  6.9 4.0 %collective-permute-start.2 = (bf16[32,2,128]{2,0,1:T(8,128)(2,1)S(1)}, bf16[32,2,128]{2,0,1:T(8,128)(2,1)S(1)}, u32[]{:S(2)}, u32[]{:S(2)}) collective-permute-start(bf16[32,2,128]{2,0,1:T(8,128)(2,1)S(1)} %get-tuple-element.39), channel_id=1, source_target_pairs={{0,1},{1,2},{2,3},{3,4},{4,5},{5,6},{6,7},{7,8},{8,9},{9,10},{10,1... | collective-permute-start | bytes 49160 | tf_op jit(solution)/shard_map/ppermute | solution.py:27
  10.9 5.5 %collective-permute-start.1 = (bf16[32,2,128]{2,0,1:T(8,128)(2,1)S(1)}, bf16[32,2,128]{2,0,1:T(8,128)(2,1)S(1)}, u32[]{:S(2)}, u32[]{:S(2)}) collective-permute-start(bf16[32,2,128]{2,0,1:T(8,128)(2,1)S(1)} %get-tuple-element.40), channel_id=1, source_target_pairs={{1,0},{2,1},{3,2},{4,3},{5,4},{6,5},{7,6},{8,7},{9,8},{10,9},{11,1... | collective-permute-start | bytes 49160 | tf_op jit(solution)/shard_map/ppermute | solution.py:30
  18.4 1.0 slice.158
  19.6 1.8 fusion.11
  24.4 9.1 %collective-permute-start.3 = (f32[2,32,24,128]{3,1,2,0:T(8,128)S(1)}, f32[2,32,24,128]{3,1,2,0:T(8,128)S(1)}, u32[]{:S(2)}, u32[]{:S(2)}) collective-permute-start(f32[2,32,24,128]{3,1,2,0:T(8,128)S(1)} %stack.88), channel_id=1, source_target_pairs={{0,256},{256,0},{16,272},{272,16},{32,288},{288,32},{48,304},{304,... | collective-permute-start | bytes 2359304 | tf_op jit(solution)/shard_map/ppermute | solution.py:42
  33.7 33.2 %collective-permute-done.3 = f32[2,32,24,128]{3,1,2,0:T(8,128)S(1)} collective-permute-done((f32[2,32,24,128]{3,1,2,0:T(8,128)S(1)}, f32[2,32,24,128]{3,1,2,0:T(8,128)S(1)}, u32[]{:S(2)}, u32[]{:S(2)}) %collective-permute-start.3) | collective-permute-done | bytes 786464 | tf_op jit(solution)/shard_map/ppermute | solution.py:42
  67.1 4.5 %collective-permute-start.4 = (f32[2,32,24,128]{3,1,2,0:T(8,128)S(1)}, f32[2,32,24,128]{3,1,2,0:T(8,128)S(1)}, u32[]{:S(2)}, u32[]{:S(2)}) collective-permute-start(f32[2,32,24,128]{3,1,2,0:T(8,128)S(1)} %pad_maximum_fusion), channel_id=1, source_target_pairs={{0,128},{128,0},{16,144},{144,16},{32,160},{160,32},{48,176},{176,... | collective-permute-start | bytes 2359304 | tf_op jit(solution)/shard_map/ppermute | solution.py:42
  71.7 35.7 %collective-permute-done.4 = f32[2,32,24,128]{3,1,2,0:T(8,128)S(1)} collective-permute-done((f32[2,32,24,128]{3,1,2,0:T(8,128)S(1)}, f32[2,32,24,128]{3,1,2,0:T(8,128)S(1)}, u32[]{:S(2)}, u32[]{:S(2)}) %collective-permute-start.4) | collective-permute-done | bytes 786464 | tf_op jit(solution)/shard_map/ppermute | solution.py:42
  107.7 2.2 collective-permute-start.5
  110.0 36.2 %collective-permute-done.5 = f32[2,32,24,128]{3,1,2,0:T(8,128)S(1)} collective-permute-done((f32[2,32,24,128]{3,1,2,0:T(8,128)S(1)}, f32[2,32,24,128]{3,1,2,0:T(8,128)S(1)}, u32[]{:S(2)}, u32[]{:S(2)}) %collective-permute-start.5) | collective-permute-done | bytes 786464 | tf_op jit(solution)/shard_map/ppermute | solution.py:42
  146.5 1.9 collective-permute-start.6
  148.6 17.8 %collective-permute-done.6 = f32[2,32,24,128]{3,1,2,0:T(8,128)S(1)} collective-permute-done((f32[2,32,24,128]{3,1,2,0:T(8,128)S(1)}, f32[2,32,24,128]{3,1,2,0:T(8,128)S(1)}, u32[]{:S(2)}, u32[]{:S(2)}) %collective-permute-start.6) | collective-permute-done | bytes 786464 | tf_op jit(solution)/shard_map/ppermute | solution.py:42
  166.7 3.8 %collective-permute-start.7 = (f32[2,32,24,128]{3,1,2,0:T(8,128)S(1)}, f32[2,32,24,128]{3,1,2,0:T(8,128)S(1)}, u32[]{:S(2)}, u32[]{:S(2)}) collective-permute-start(f32[2,32,24,128]{3,1,2,0:T(8,128)S(1)} %pad_maximum_fusion.3), channel_id=1, source_target_pairs={{0,16},{16,0},{32,48},{48,32},{64,80},{80,64},{96,112},{112,96},{1... | collective-permute-start | bytes 2359304 | tf_op jit(solution)/shard_map/ppermute | solution.py:42
  170.7 1.7 collective-permute-done.7
  176.0 5.4 %collective-permute-start.8 = (bf16[64,2,128]{2,0,1:T(8,128)(2,1)S(1)}, bf16[64,2,128]{2,0,1:T(8,128)(2,1)S(1)}, u32[]{:S(2)}, u32[]{:S(2)}) collective-permute-start(bf16[64,2,128]{2,0,1:T(8,128)(2,1)S(1)} %get-tuple-element.35), channel_id=1, source_target_pairs={{1,0},{2,1},{3,2},{4,3},{5,4},{6,5},{7,6},{8,7},{9,8},{10,9},{11,1... | collective-permute-start | bytes 98312 | tf_op jit(solution)/shard_map/ppermute | solution.py:30
  181.5 2.1 collective-permute-start.9
  183.6 5.2 %collective-permute-done.9 = bf16[64,2,128]{2,0,1:T(8,128)(2,1)S(1)} collective-permute-done((bf16[64,2,128]{2,0,1:T(8,128)(2,1)S(1)}, bf16[64,2,128]{2,0,1:T(8,128)(2,1)S(1)}, u32[]{:S(2)}, u32[]{:S(2)}) %collective-permute-start.9) | collective-permute-done | bytes 32800 | tf_op jit(solution)/shard_map/ppermute | solution.py:27
  190.1 0.9 convolution_add_fusion.3
  192.9 0.9 fusion
  197.4 3.7 %collective-permute-start.10 = (f32[2,32,24,128]{3,1,2,0:T(8,128)S(1)}, f32[2,32,24,128]{3,1,2,0:T(8,128)S(1)}, u32[]{:S(2)}, u32[]{:S(2)}) collective-permute-start(f32[2,32,24,128]{3,1,2,0:T(8,128)S(1)} %pad_maximum_fusion.4), channel_id=1, source_target_pairs={{0,16},{16,0},{32,48},{48,32},{64,80},{80,64},{96,112},{112,96},{1... | collective-permute-start | bytes 2359304 | tf_op jit(solution)/shard_map/ppermute | solution.py:42
  201.2 1.9 collective-permute-done.10
  203.4 1.9 collective-permute-start.11
  205.3 18.7 %collective-permute-done.11 = f32[2,32,24,128]{3,1,2,0:T(8,128)S(1)} collective-permute-done((f32[2,32,24,128]{3,1,2,0:T(8,128)S(1)}, f32[2,32,24,128]{3,1,2,0:T(8,128)S(1)}, u32[]{:S(2)}, u32[]{:S(2)}) %collective-permute-start.11) | collective-permute-done | bytes 786464 | tf_op jit(solution)/shard_map/ppermute | solution.py:42
  224.3 1.9 collective-permute-start.12
  226.3 36.9 %collective-permute-done.12 = f32[2,32,24,128]{3,1,2,0:T(8,128)S(1)} collective-permute-done((f32[2,32,24,128]{3,1,2,0:T(8,128)S(1)}, f32[2,32,24,128]{3,1,2,0:T(8,128)S(1)}, u32[]{:S(2)}, u32[]{:S(2)}) %collective-permute-start.12) | collective-permute-done | bytes 786464 | tf_op jit(solution)/shard_map/ppermute | solution.py:42
  263.5 2.7 collective-permute-start.13
  266.2 36.9 %collective-permute-done.13 = f32[2,32,24,128]{3,1,2,0:T(8,128)S(1)} collective-permute-done((f32[2,32,24,128]{3,1,2,0:T(8,128)S(1)}, f32[2,32,24,128]{3,1,2,0:T(8,128)S(1)}, u32[]{:S(2)}, u32[]{:S(2)}) %collective-permute-start.13) | collective-permute-done | bytes 786464 | tf_op jit(solution)/shard_map/ppermute | solution.py:42
  303.5 3.7 %collective-permute-start.14 = (f32[2,32,24,128]{3,1,2,0:T(8,128)S(1)}, f32[2,32,24,128]{3,1,2,0:T(8,128)S(1)}, u32[]{:S(2)}, u32[]{:S(2)}) collective-permute-start(f32[2,32,24,128]{3,1,2,0:T(8,128)S(1)} %pad_maximum_fusion.8), channel_id=1, source_target_pairs={{0,256},{256,0},{16,272},{272,16},{32,288},{288,32},{48,304},{304,... | collective-permute-start | bytes 2359304 | tf_op jit(solution)/shard_map/ppermute | solution.py:42
  307.3 36.2 %collective-permute-done.14 = f32[2,32,24,128]{3,1,2,0:T(8,128)S(1)} collective-permute-done((f32[2,32,24,128]{3,1,2,0:T(8,128)S(1)}, f32[2,32,24,128]{3,1,2,0:T(8,128)S(1)}, u32[]{:S(2)}, u32[]{:S(2)}) %collective-permute-start.14) | collective-permute-done | bytes 786464 | tf_op jit(solution)/shard_map/ppermute | solution.py:42
  343.8 1.0 copy.18
  (154 shorter events, 18.1 us)
Async XLA Ops:
  0.0 175.1 %copy-start = (bf16[24,128,128]{2,1,0:T(8,128)(2,1)S(1)}, bf16[24,128,128]{2,1,0:T(8,128)(2,1)}, u32[]{:S(2)}) copy-start(bf16[24,128,128]{2,1,0:T(8,128)(2,1)} %param.10) | copy-start | bytes 2359300
  0.8 18.7 %collective-permute-start = (f32[1,24,128]{2,0,1:T(1,128)S(1)}, f32[1,24,128]{2,0,1:T(1,128)S(1)}, u32[]{:S(2)}, u32[]{:S(2)}) collective-permute-start(f32[1,24,128]{2,0,1:T(1,128)S(1)} %bitcast.328), channel_id=1, source_target_pairs={{0,16},{16,32},{32,48},{48,64},{64,80},{80,96},{96,112},{112,128},... | collective-permute-start | bytes 36872 | tf_op jit(solution)/shard_map/ppermute | solution.py:19
  6.9 12.7 %collective-permute-start.2 = (bf16[32,2,128]{2,0,1:T(8,128)(2,1)S(1)}, bf16[32,2,128]{2,0,1:T(8,128)(2,1)S(1)}, u32[]{:S(2)}, u32[]{:S(2)}) collective-permute-start(bf16[32,2,128]{2,0,1:T(8,128)(2,1)S(1)} %get-tuple-element.39), channel_id=1, source_target_pairs={{0,1},{1,2},{2,3},{3,4},{4,5},{5,6},{6,7},{7,8},{8,9},{9,10},{10,1... | collective-permute-start | bytes 49160 | tf_op jit(solution)/shard_map/ppermute | solution.py:27
  10.9 8.7 %collective-permute-start.1 = (bf16[32,2,128]{2,0,1:T(8,128)(2,1)S(1)}, bf16[32,2,128]{2,0,1:T(8,128)(2,1)S(1)}, u32[]{:S(2)}, u32[]{:S(2)}) collective-permute-start(bf16[32,2,128]{2,0,1:T(8,128)(2,1)S(1)} %get-tuple-element.40), channel_id=1, source_target_pairs={{1,0},{2,1},{3,2},{4,3},{5,4},{6,5},{7,6},{8,7},{9,8},{10,9},{11,1... | collective-permute-start | bytes 49160 | tf_op jit(solution)/shard_map/ppermute | solution.py:30
  17.3 5.6 %copy-start.38 = (pred[24]{0:T(512)(128)(4,1)}, pred[24]{0:T(512)(128)(4,1)S(1)}, u32[]{:S(2)}) copy-start(pred[24]{0:T(512)(128)(4,1)S(1)} %get-tuple-element.62) | copy-start | bytes 76
  17.3 5.7 %copy-start.42 = (pred[24]{0:T(512)(128)(4,1)}, pred[24]{0:T(512)(128)(4,1)S(1)}, u32[]{:S(2)}) copy-start(pred[24]{0:T(512)(128)(4,1)S(1)} %get-tuple-element.63) | copy-start | bytes 76
  17.3 5.8 %copy-start.36 = (pred[24]{0:T(512)(128)(4,1)}, pred[24]{0:T(512)(128)(4,1)S(1)}, u32[]{:S(2)}) copy-start(pred[24]{0:T(512)(128)(4,1)S(1)} %get-tuple-element.65) | copy-start | bytes 76
  17.3 6.4 %copy-start.32 = (pred[24]{0:T(512)(128)(4,1)}, pred[24]{0:T(512)(128)(4,1)S(1)}, u32[]{:S(2)}) copy-start(pred[24]{0:T(512)(128)(4,1)S(1)} %get-tuple-element.60) | copy-start | bytes 76
  17.3 6.4 %copy-start.34 = (pred[24]{0:T(512)(128)(4,1)}, pred[24]{0:T(512)(128)(4,1)S(1)}, u32[]{:S(2)}) copy-start(pred[24]{0:T(512)(128)(4,1)S(1)} %get-tuple-element.61) | copy-start | bytes 76
  24.4 42.5 %collective-permute-start.3 = (f32[2,32,24,128]{3,1,2,0:T(8,128)S(1)}, f32[2,32,24,128]{3,1,2,0:T(8,128)S(1)}, u32[]{:S(2)}, u32[]{:S(2)}) collective-permute-start(f32[2,32,24,128]{3,1,2,0:T(8,128)S(1)} %stack.88), channel_id=1, source_target_pairs={{0,256},{256,0},{16,272},{272,16},{32,288},{288,32},{48,304},{304,... | collective-permute-start | bytes 2359304 | tf_op jit(solution)/shard_map/ppermute | solution.py:42
  67.1 40.4 %collective-permute-start.4 = (f32[2,32,24,128]{3,1,2,0:T(8,128)S(1)}, f32[2,32,24,128]{3,1,2,0:T(8,128)S(1)}, u32[]{:S(2)}, u32[]{:S(2)}) collective-permute-start(f32[2,32,24,128]{3,1,2,0:T(8,128)S(1)} %pad_maximum_fusion), channel_id=1, source_target_pairs={{0,128},{128,0},{16,144},{144,16},{32,160},{160,32},{48,176},{176,... | collective-permute-start | bytes 2359304 | tf_op jit(solution)/shard_map/ppermute | solution.py:42
  107.7 38.5 %collective-permute-start.5 = (f32[2,32,24,128]{3,1,2,0:T(8,128)S(1)}, f32[2,32,24,128]{3,1,2,0:T(8,128)S(1)}, u32[]{:S(2)}, u32[]{:S(2)}) collective-permute-start(f32[2,32,24,128]{3,1,2,0:T(8,128)S(1)} %pad_maximum_fusion.1), channel_id=1, source_target_pairs={{0,64},{64,0},{16,80},{80,16},{32,96},{96,32},{48,112},{112,48},{1... | collective-permute-start | bytes 2359304 | tf_op jit(solution)/shard_map/ppermute | solution.py:42
  146.5 19.9 %collective-permute-start.6 = (f32[2,32,24,128]{3,1,2,0:T(8,128)S(1)}, f32[2,32,24,128]{3,1,2,0:T(8,128)S(1)}, u32[]{:S(2)}, u32[]{:S(2)}) collective-permute-start(f32[2,32,24,128]{3,1,2,0:T(8,128)S(1)} %pad_maximum_fusion.2), channel_id=1, source_target_pairs={{0,32},{32,0},{16,48},{48,16},{64,96},{96,64},{80,112},{112,80},{1... | collective-permute-start | bytes 2359304 | tf_op jit(solution)/shard_map/ppermute | solution.py:42
  166.7 5.7 %collective-permute-start.7 = (f32[2,32,24,128]{3,1,2,0:T(8,128)S(1)}, f32[2,32,24,128]{3,1,2,0:T(8,128)S(1)}, u32[]{:S(2)}, u32[]{:S(2)}) collective-permute-start(f32[2,32,24,128]{3,1,2,0:T(8,128)S(1)} %pad_maximum_fusion.3), channel_id=1, source_target_pairs={{0,16},{16,0},{32,48},{48,32},{64,80},{80,64},{96,112},{112,96},{1... | collective-permute-start | bytes 2359304 | tf_op jit(solution)/shard_map/ppermute | solution.py:42
  173.8 15.2 %copy-start.25 = (pred[24]{0:T(512)(128)(4,1)S(1)}, pred[24]{0:T(512)(128)(4,1)}, u32[]{:S(2)}) copy-start(pred[24]{0:T(512)(128)(4,1)} %copy-done.24) | copy-start | bytes 76
  173.8 15.2 %copy-start.27 = (pred[24]{0:T(512)(128)(4,1)S(1)}, pred[24]{0:T(512)(128)(4,1)}, u32[]{:S(2)}) copy-start(pred[24]{0:T(512)(128)(4,1)} %copy-done.26) | copy-start | bytes 76
  173.8 15.2 %copy-start.29 = (pred[24]{0:T(512)(128)(4,1)S(1)}, pred[24]{0:T(512)(128)(4,1)}, u32[]{:S(2)}) copy-start(pred[24]{0:T(512)(128)(4,1)} %copy-done.28) | copy-start | bytes 76
  173.8 15.2 %copy-start.31 = (pred[24]{0:T(512)(128)(4,1)S(1)}, pred[24]{0:T(512)(128)(4,1)}, u32[]{:S(2)}) copy-start(pred[24]{0:T(512)(128)(4,1)} %copy-done.30) | copy-start | bytes 76
  173.9 15.2 %copy-start.43 = (pred[24]{0:T(512)(128)(4,1)S(1)}, pred[24]{0:T(512)(128)(4,1)}, u32[]{:S(2)}) copy-start(pred[24]{0:T(512)(128)(4,1)} %copy-done.42) | copy-start | bytes 76
  173.9 15.2 %copy-start.45 = (bf16[5,24,128,128]{3,2,1,0:T(8,128)(2,1)S(1)}, bf16[5,24,128,128]{3,2,1,0:T(8,128)(2,1)}, u32[]{:S(2)}) copy-start(bf16[5,24,128,128]{3,2,1,0:T(8,128)(2,1)} %param.9) | copy-start | bytes 11796484
  175.8 14.3 %copy-start.17 = (pred[24]{0:T(512)(128)(4,1)S(1)}, pred[24]{0:T(512)(128)(4,1)}, u32[]{:S(2)}) copy-start(pred[24]{0:T(512)(128)(4,1)} %copy-done.16) | copy-start | bytes 76
  175.8 14.3 %copy-start.19 = (pred[24]{0:T(512)(128)(4,1)S(1)}, pred[24]{0:T(512)(128)(4,1)}, u32[]{:S(2)}) copy-start(pred[24]{0:T(512)(128)(4,1)} %copy-done.18) | copy-start | bytes 76
  175.8 14.3 %copy-start.21 = (pred[24]{0:T(512)(128)(4,1)S(1)}, pred[24]{0:T(512)(128)(4,1)}, u32[]{:S(2)}) copy-start(pred[24]{0:T(512)(128)(4,1)} %copy-done.20) | copy-start | bytes 76
  175.8 14.3 %copy-start.23 = (pred[24]{0:T(512)(128)(4,1)S(1)}, pred[24]{0:T(512)(128)(4,1)}, u32[]{:S(2)}) copy-start(pred[24]{0:T(512)(128)(4,1)} %copy-done.22) | copy-start | bytes 76
  175.8 14.3 %copy-start.41 = (pred[24]{0:T(512)(128)(4,1)S(1)}, pred[24]{0:T(512)(128)(4,1)}, u32[]{:S(2)}) copy-start(pred[24]{0:T(512)(128)(4,1)} %copy-done.40) | copy-start | bytes 76
  176.0 7.5 %collective-permute-start.8 = (bf16[64,2,128]{2,0,1:T(8,128)(2,1)S(1)}, bf16[64,2,128]{2,0,1:T(8,128)(2,1)S(1)}, u32[]{:S(2)}, u32[]{:S(2)}) collective-permute-start(bf16[64,2,128]{2,0,1:T(8,128)(2,1)S(1)} %get-tuple-element.35), channel_id=1, source_target_pairs={{1,0},{2,1},{3,2},{4,3},{5,4},{6,5},{7,6},{8,7},{9,8},{10,9},{11,1... | collective-permute-start | bytes 98312 | tf_op jit(solution)/shard_map/ppermute | solution.py:30
  181.5 7.4 %collective-permute-start.9 = (bf16[64,2,128]{2,0,1:T(8,128)(2,1)S(1)}, bf16[64,2,128]{2,0,1:T(8,128)(2,1)S(1)}, u32[]{:S(2)}, u32[]{:S(2)}) collective-permute-start(bf16[64,2,128]{2,0,1:T(8,128)(2,1)S(1)} %get-tuple-element.36), channel_id=1, source_target_pairs={{0,1},{1,2},{2,3},{3,4},{4,5},{5,6},{6,7},{7,8},{8,9},{9,10},{10,1... | collective-permute-start | bytes 98312 | tf_op jit(solution)/shard_map/ppermute | solution.py:27
  197.4 5.6 %collective-permute-start.10 = (f32[2,32,24,128]{3,1,2,0:T(8,128)S(1)}, f32[2,32,24,128]{3,1,2,0:T(8,128)S(1)}, u32[]{:S(2)}, u32[]{:S(2)}) collective-permute-start(f32[2,32,24,128]{3,1,2,0:T(8,128)S(1)} %pad_maximum_fusion.4), channel_id=1, source_target_pairs={{0,16},{16,0},{32,48},{48,32},{64,80},{80,64},{96,112},{112,96},{1... | collective-permute-start | bytes 2359304 | tf_op jit(solution)/shard_map/ppermute | solution.py:42
  203.4 20.6 %collective-permute-start.11 = (f32[2,32,24,128]{3,1,2,0:T(8,128)S(1)}, f32[2,32,24,128]{3,1,2,0:T(8,128)S(1)}, u32[]{:S(2)}, u32[]{:S(2)}) collective-permute-start(f32[2,32,24,128]{3,1,2,0:T(8,128)S(1)} %pad_maximum_fusion.5), channel_id=1, source_target_pairs={{0,32},{32,0},{16,48},{48,16},{64,96},{96,64},{80,112},{112,80},{1... | collective-permute-start | bytes 2359304 | tf_op jit(solution)/shard_map/ppermute | solution.py:42
  224.3 38.8 %collective-permute-start.12 = (f32[2,32,24,128]{3,1,2,0:T(8,128)S(1)}, f32[2,32,24,128]{3,1,2,0:T(8,128)S(1)}, u32[]{:S(2)}, u32[]{:S(2)}) collective-permute-start(f32[2,32,24,128]{3,1,2,0:T(8,128)S(1)} %pad_maximum_fusion.6), channel_id=1, source_target_pairs={{0,64},{64,0},{16,80},{80,16},{32,96},{96,32},{48,112},{112,48},{1... | collective-permute-start | bytes 2359304 | tf_op jit(solution)/shard_map/ppermute | solution.py:42
  263.5 39.6 %collective-permute-start.13 = (f32[2,32,24,128]{3,1,2,0:T(8,128)S(1)}, f32[2,32,24,128]{3,1,2,0:T(8,128)S(1)}, u32[]{:S(2)}, u32[]{:S(2)}) collective-permute-start(f32[2,32,24,128]{3,1,2,0:T(8,128)S(1)} %pad_maximum_fusion.7), channel_id=1, source_target_pairs={{0,128},{128,0},{16,144},{144,16},{32,160},{160,32},{48,176},{176,... | collective-permute-start | bytes 2359304 | tf_op jit(solution)/shard_map/ppermute | solution.py:42
  303.5 40.0 %collective-permute-start.14 = (f32[2,32,24,128]{3,1,2,0:T(8,128)S(1)}, f32[2,32,24,128]{3,1,2,0:T(8,128)S(1)}, u32[]{:S(2)}, u32[]{:S(2)}) collective-permute-start(f32[2,32,24,128]{3,1,2,0:T(8,128)S(1)} %pad_maximum_fusion.8), channel_id=1, source_target_pairs={{0,256},{256,0},{16,272},{272,16},{32,288},{288,32},{48,304},{304,... | collective-permute-start | bytes 2359304 | tf_op jit(solution)/shard_map/ppermute | solution.py:42
  (30 other events, 103.7 us)
where the time goes:
time: 345 us
  waiting for transfers between devices  261 us (76%)
  starting transfers between devices  57.4 us (17%)
  matrix products  14.5 us (4%)
  other arithmetic  6.81 us (2%)
  local copies, waits for them, and re-layouts  3.47 us (1%)
    ppermute x10, waiting for transfers between devices, from_partner(): return lax.ppermute(block, axis, route)  255 us
    ppermute x10, starting transfers between devices, from_partner(): return lax.ppermute(block, axis, route)  35.5 us
    ppermute x2, starting transfers between devices, extended(): lax.ppermute(lax.slice_in_dim(block, 0, width, axis=dim), axis, backward)  10.9 us
    dot_general x10, matrix products, apply_padded(): jnp.einsum('fbj,bij->fbi', chosen, blocks[column], preferred_element_type...  8.59 us
  transfers between devices with their start and end apart: 15, of which 11 were waited for; matrix products, arithmetic and copies ran while one was open for 1% of the time, Pallas kernels for 0%

commit v1 on v0

v1 whole, which is shorter than its diff:
```python
import math

import jax
import jax.numpy as jnp
from jax import lax
from jax.sharding import PartitionSpec as P

alpha_rate = 0.5
time_step = 0.5
relaxation = 0.7
GROUP = 8


def exchange(low_edge, high_edge, axis):
    count = lax.axis_size(axis)
    odd = (lax.axis_index(axis) & 1) == 1
    first, second = [], []
    for i in range(count - 1):
        (first if i & 1 else second).extend([(i, i + 1), (i + 1, i)])
    got_first = lax.ppermute(jnp.where(odd, high_edge, low_edge), axis, first)
    got_second = lax.ppermute(jnp.where(odd, low_edge, high_edge), axis, second)
    low = jnp.where(odd, got_second, got_first)
    high = jnp.where(odd, got_first, got_second)
    return low, high


def extended(block):
    low, high = exchange(block[:, :2], block[:, -2:], "space")
    return jnp.concatenate([low, block, high], axis=1)


def apply_padded(padded, blocks, couple):
    width = padded.shape[1] - 4
    total = None
    for column in range(5):
        chosen = padded[:, 2 : 2 + width]
        for offset in range(-2, 3):
            picked = (couple[:, column] == offset)[None, :, None]
            chosen = jnp.where(picked, padded[:, 2 + offset : 2 + offset + width], chosen)
        term = jnp.einsum(
            "fbj,bij->fbi", chosen, blocks[column], preferred_element_type=jnp.float32
        )
        total = term if total is None else total + term
    return total


def split(value):
    high = lax.reduce_precision(value, 8, 7)
    return high.astype(jnp.bfloat16), (value - high).astype(jnp.bfloat16)


def step_matrix(power, steps):
    scale = jnp.exp2(-float(steps) * power)
    return scale, scale * (0.5 * steps) * power


def carried(power, steps, value):
    scale, couple = step_matrix(power, steps)
    return jnp.stack([scale * value[0] + couple * value[1], scale * value[1]])


def ring_carry(ends, steps):
    count = lax.axis_size("tm")
    position = lax.axis_index("tm")
    groups = count // GROUP
    inner = [[g * GROUP + i for i in range(GROUP)] for g in range(groups)]
    outer = [[g * GROUP + i for g in range(groups)] for i in range(GROUP)]
    mine = position % GROUP
    group = position // GROUP
    sent = jnp.broadcast_to(ends.astype(jnp.bfloat16)[None], (GROUP,) + ends.shape)
    got = lax.all_to_all(sent, "tm", 0, 0, axis_index_groups=inner, tiled=True)
    got = got.astype(jnp.float32)
    total = jnp.zeros_like(ends)
    before = jnp.zeros_like(ends)
    for i in range(GROUP):
        total = total + carried(jnp.float32(GROUP - 1 - i), steps, got[i])
        power = (mine - 1 - i).astype(jnp.float32)
        part = carried(jnp.maximum(power, 0.0), steps, got[i])
        before = before + jnp.where(power >= 0, part, 0.0)
    sent = jnp.broadcast_to(total.astype(jnp.bfloat16)[None], (groups,) + ends.shape)
    got = lax.all_to_all(sent, "tm", 0, 0, axis_index_groups=outer, tiled=True)
    got = got.astype(jnp.float32)
    into = jnp.zeros_like(ends)
    for g in range(groups):
        distance = (group - 1 - g) % groups
        wrapped = jnp.where(g >= group, alpha_rate, 1.0)
        part = carried((GROUP * distance).astype(jnp.float32), steps, got[g])
        into = into + wrapped * part
    closing = 1.0 / (1.0 - alpha_rate * 2.0 ** (-steps * count))
    return before + carried(mine.astype(jnp.float32), steps, closing * into)


def on_device(state, forcing, initial, blocks, precond, couple):
    steps = state.shape[0]
    position = lax.axis_index("tm")
    count = lax.axis_size("tm")
    squares = (0.5 * state * state).astype(jnp.bfloat16)
    flux = apply_padded(extended(squares), blocks, couple)
    first = jnp.where(position == 0, initial, 0.0)[None]
    residual = forcing - state + jnp.concatenate([first, state[:-1]], 0) - time_step * flux
    onward = jnp.where(position == count - 1, 0.0, state[-1:])
    rows = jnp.concatenate([residual, onward], 0)
    smooth = jnp.einsum(
        "fbj,bij->fbi", rows.astype(jnp.bfloat16), precond, preferred_element_type=jnp.float32
    )
    outer = 2.0 * rows - relaxation * smooth
    coupled = apply_padded(extended(smooth.astype(jnp.bfloat16)), blocks, couple)
    inner = relaxation * (smooth - time_step * coupled)
    pieces = jnp.concatenate(split(outer) + split(inner), 0)
    solved = jnp.einsum("fbj,bij->fbi", pieces, precond, preferred_element_type=jnp.float32)
    solved = solved.reshape((2, 2) + rows.shape).sum(1)
    lag = jnp.arange(steps)[:, None] - jnp.arange(steps)[None, :]
    once = jnp.where(lag >= 0, jnp.exp2(-(lag + 1.0)), 0.0)
    highest = lax.Precision.HIGHEST
    z = jnp.einsum("nm,mbc->nbc", once, solved[1, :steps], precision=highest)
    y = jnp.einsum("nm,mbc->nbc", once, solved[0, :steps] + z, precision=highest)
    ends = jnp.stack([y[-1] + solved[0, steps], z[-1] + solved[1, steps]])
    carry = ring_carry(ends, steps)
    index = jnp.arange(1, steps + 1, dtype=jnp.float32)[:, None, None]
    y = y + jnp.exp2(-index) * (carry[0] + 0.5 * index * carry[1])
    return state + relaxation * y


def solution(mesh):
    placed = (
        P("tm", "space", None),
        P("tm", "space", None),
        P("space", None),
        P(None, "space", None, None),
        P("space", None, None),
        P("space", None),
    )
    return jax.shard_map(
        on_device, mesh=mesh, in_specs=placed, out_specs=P("tm", "space", None), check_vma=False
    )
```

time: 345 us -> 77.1 us (0.22)
  the two profiles are of different devices: /device:TPU:27 before, /device:TPU:6 now
where the time goes in v1:
time: 77.1 us; the launch traced here: 76.2 us
  starting transfers between devices  31.7 us (41%)
  waiting for transfers between devices  20.8 us (27%)
  matrix products  9.42 us (12%)
  other arithmetic  7.74 us (10%)
  local copies, waits for them, and re-layouts  5.59 us (7%)
  between operations  1.01 us (1%)
    all_to_all x1, waiting for transfers between devices, ring_carry(): got = lax.all_to_all(sent, 'tm', 0, 0, axis_index_groups=outer, tiled=True)  12.7 us
    all_to_all x1, starting transfers between devices, ring_carry(): got = lax.all_to_all(sent, 'tm', 0, 0, axis_index_groups=outer, tiled=True)  11.6 us
    ppermute x2, starting transfers between devices, exchange(): got_first = lax.ppermute(jnp.where(odd, high_edge, low_edge), axis, first)  10.1 us
    dot_general x10, matrix products, apply_padded(): jnp.einsum('fbj,bij->fbi', chosen, blocks[column], preferred_element_type...  7.19 us
    ppermute x2, starting transfers between devices, exchange(): got_second = lax.ppermute(jnp.where(odd, low_edge, high_edge), axis, second)  5.84 us
    all_to_all x1, waiting for transfers between devices, ring_carry(): got = lax.all_to_all(sent, 'tm', 0, 0, axis_index_groups=inner, tiled=True)  5.66 us
    all_to_all x1, starting transfers between devices, ring_carry(): got = lax.all_to_all(sent, 'tm', 0, 0, axis_index_groups=inner, tiled=True)  4.12 us
    ppermute x2, waiting for transfers between devices, exchange(): got_first = lax.ppermute(jnp.where(odd, high_edge, low_edge), axis, first)  2.52 us
  transfers between devices with their start and end apart: 6, of which 3 were waited for; matrix products, arithmetic and copies ran while one was open for 6% of the time, Pallas kernels for 0%

profile of v1, /device:TPU:6, one launch (start us, length us, event | category | flops | bytes accessed | tf_op | source)
XLA Modules:
  0.0 76.2 jit_solution(6929852366243214975)
XLA Ops:
  0.0 1.1 %fusion.39 = bf16[32,24,128]{2,1,0:T(8,128)(2,1)S(1)} fusion(f32[32,24,128]{2,1,0:T(8,128)} %param.6), kind=kLoop, calls=%fused_computation.55 | loop fusion | flops 294912 | bytes 589824 | tf_op jit(solution)/shard_map/convert_element_type | solution.py:97
  1.2 8.2 %collective-permute-start = (bf16[32,2,128]{2,1,0:T(2,128)(2,1)S(1)}, bf16[32,2,128]{2,1,0:T(2,128)(2,1)S(1)}, u32[]{:S(2)}, u32[]{:S(2)}) collective-permute-start(bf16[32,2,128]{2,1,0:T(2,128)(2,1)S(1)} %get-tuple-element.52), channel_id=1, source_target_pairs={{1,2},{2,1},{3,4},{4,3},{5,6},{6,5},{7,8},{8,7},{9,10},{10,9},{11,... | collective-permute-start | bytes 49160 | tf_op jit(solution)/shard_map/ppermute | solution.py:20
  9.3 1.9 %collective-permute-start.1 = (bf16[32,2,128]{2,1,0:T(2,128)(2,1)S(1)}, bf16[32,2,128]{2,1,0:T(2,128)(2,1)S(1)}, u32[]{:S(2)}, u32[]{:S(2)}) collective-permute-start(bf16[32,2,128]{2,1,0:T(2,128)(2,1)S(1)} %get-tuple-element.53), channel_id=1, source_target_pairs={{0,1},{1,0},{2,3},{3,2},{4,5},{5,4},{6,7},{7,6},{8,9},{9,8},{10,11... | collective-permute-start | bytes 49160 | tf_op jit(solution)/shard_map/ppermute | solution.py:21
  11.3 0.9 %compare_bitcast_fusion.9 = (pred[24]{0:T(512)(128)(4,1)S(1)}, pred[24]{0:T(512)(128)(4,1)S(1)}, pred[24]{0:T(512)(128)(4,1)S(1)}, pred[24]{0:T(512)(128)(4,1)S(...) fusion(s32[24,5]{0,1:T(8,128)} %param.11), kind=kLoop, calls=%fused_computation.288 | loop fusion | flops 456 | bytes 936 | tf_op jit(solution)/shard_map/eq | solution.py:38
  12.2 0.9 %slice_select_fusion = f32[1,24,128]{2,1,0:T(8,128)S(1)} fusion(f32[32,24,128]{2,1,0:T(8,128)} %param.6, pred[]{:T(512)S(6)} %eq.343), kind=kLoop, calls=%fused_computation.263 | loop fusion | flops 3072 | bytes 24577 | tf_op jit(solution)/shard_map/jit(_where)/select_n | solution.py:101
  13.0 0.9 %broadcast_select_fusion.8 = f32[24,128]{1,0:T(8,128)S(1)} fusion(f32[24,128]{1,0:T(8,128)} %param.8, pred[]{:T(512)S(6)} %eq.291), kind=kLoop, calls=%fused_computation.278 | loop fusion | flops 3072 | bytes 24577 | tf_op jit(solution)/shard_map/jit(_where)/select_n | solution.py:99
  14.0 0.8 %compare_bitcast_fusion.14 = (pred[24]{0:T(512)(128)(4,1)S(1)}, pred[24]{0:T(512)(128)(4,1)S(1)}, pred[24]{0:T(512)(128)(4,1)S(1)}, pred[24]{0:T(512)(128)(4,1)S...) fusion(s32[24,5]{0,1:T(8,128)} %param.11), kind=kLoop, calls=%fused_computation.293 | loop fusion | flops 144 | bytes 528 | tf_op jit(solution)/shard_map/eq | solution.py:38
  14.8 1.0 %slice.427 = f32[31,24,128]{2,1,0:T(8,128)S(1)} slice(f32[32,24,128]{2,1,0:T(8,128)} %param.6), slice={[0:31], [0:24], [0:128]} | slice | bytes 761856 | tf_op jit(solution)/shard_map/slice | solution.py:100
  16.5 1.6 %fusion.24 = f32[24,32,128]{2,1,0:T(8,128)S(1)} fusion(bf16[5,24,128,128]{3,2,1,0:T(8,128)(2,1)} %param.9, bf16[32,24,128]{2,1,0:T(8,128)(2,1)S(1)} %fusion.122), kind=kOutput, calls=%fused_computation.33 | convolution fusion | flops 25165824 | bytes 1376256 | tf_op jit(solution)/shard_map/fbj,bij->fbi/dot_general | solution.py:40
  18.5 0.5 convolution_add_fusion.7
  19.3 0.5 convolution_add_fusion.6
  20.6 0.5 fusion.6
  21.1 0.7 reduce-precision_convert_fusion.1
  21.9 1.9 %collective-permute-start.2 = (bf16[33,2,128]{2,0,1:T(8,128)(2,1)S(1)}, bf16[33,2,128]{2,0,1:T(8,128)(2,1)S(1)}, u32[]{:S(2)}, u32[]{:S(2)}) collective-permute-start(bf16[33,2,128]{2,0,1:T(8,128)(2,1)S(1)} %get-tuple-element.19), channel_id=1, source_target_pairs={{1,2},{2,1},{3,4},{4,3},{5,6},{6,5},{7,8},{8,7},{9,10},{10,9},{11,... | collective-permute-start | bytes 50696 | tf_op jit(solution)/shard_map/ppermute | solution.py:20
  23.8 3.9 %collective-permute-start.3 = (bf16[33,2,128]{2,0,1:T(8,128)(2,1)S(1)}, bf16[33,2,128]{2,0,1:T(8,128)(2,1)S(1)}, u32[]{:S(2)}, u32[]{:S(2)}) collective-permute-start(bf16[33,2,128]{2,0,1:T(8,128)(2,1)S(1)} %get-tuple-element.18), channel_id=1, source_target_pairs={{0,1},{1,0},{2,3},{3,2},{4,5},{5,4},{6,7},{7,6},{8,9},{9,8},{10,11... | collective-permute-start | bytes 50696 | tf_op jit(solution)/shard_map/ppermute | solution.py:21
  27.7 2.5 %collective-permute-done.2 = bf16[33,2,128]{2,0,1:T(8,128)(2,1)S(1)} collective-permute-done((bf16[33,2,128]{2,0,1:T(8,128)(2,1)S(1)}, bf16[33,2,128]{2,0,1:T(8,128)(2,1)S(1)}, u32[]{:S(2)}, u32[]{:S(2)}) %collective-permute-start.2) | collective-permute-done | bytes 16928 | tf_op jit(solution)/shard_map/ppermute | solution.py:20
  30.3 0.7 fusion.22
  31.0 0.7 convolution_add_fusion.3
  31.7 0.7 convolution_add_fusion.2
  32.4 0.7 convolution_add_fusion.1
  33.1 0.7 reduce-precision_convert_fusion
  33.8 0.6 convolution_bitcast_fusion
  34.8 1.1 %reduce_sum.9 = f32[2,33,24,128]{3,2,1,0:T(8,128)} reduce(f32[2,2,33,24,128]{4,3,2,1,0:T(8,128)S(1)} %bitcast.203, f32[]{:T(128)} %constant.123.clone.1), dimensions={1}, to_apply=%region_0.1 | reduce | flops 202752 | bytes 2433028 | tf_op jit(solution)/shard_map/reduce_sum | solution.py:111
  35.9 1.2 %fusion.201 = (f32[1,32,24,128]{3,2,1,0:T(8,128)S(1)}, f32[1,32,24,128]{3,2,1,0:T(8,128)S(1)}) fusion(f32[2,33,24,128]{3,2,1,0:T(8,128)} %reduce_sum.9), kind=kLoop, calls=%fused_computation.323 | loop fusion | bytes 1572864 | tf_op jit(solution)/shard_map/slice | solution.py:116
  37.0 0.7 fusion.200
  38.8 0.7 broadcast_in_dim.403
  39.5 4.1 %all-to-all-start = ((bf16[8,2,24,128]{3,2,1,0:T(8,128)(2,1)}), bf16[8,2,24,128]{3,2,1,0:T(8,128)(2,1)S(1)}, u32[]{:S(2)}, u32[]{:S(2)}) async-start(bf16[8,2,24,128]{3,2,1,0:T(8,128)(2,1)} %broadcast_in_dim.403), calls=%async_computation | async-start | bytes 196608 | tf_op jit(solution)/shard_map/all_to_all | solution.py:71
  44.3 5.7 %all-to-all-done = bf16[8,2,24,128]{3,2,1,0:T(8,128)(2,1)S(1)} async-done(((bf16[8,2,24,128]{3,2,1,0:T(8,128)(2,1)}), bf16[8,2,24,128]{3,2,1,0:T(8,128)(2,1)S(1)}, u32[]{:S(2)}, u32[]{:S(2)}) %all-to-all-start) | async-done | bytes 98336 | tf_op jit(solution)/shard_map/all_to_all | solution.py:71
  50.0 0.6 broadcast_in_dim.406
  50.6 11.6 %all-to-all-start.1 = ((bf16[4,2,24,128]{3,2,1,0:T(8,128)(2,1)}), bf16[4,2,24,128]{3,2,1,0:T(8,128)(2,1)S(1)}, u32[]{:S(2)}, u32[]{:S(2)}) async-start(bf16[4,2,24,128]{3,2,1,0:T(8,128)(2,1)} %broadcast_in_dim.406), calls=%async_computation.1 | async-start | bytes 98304 | tf_op jit(solution)/shard_map/all_to_all | solution.py:81
  62.3 12.7 %all-to-all-done.1 = bf16[4,2,24,128]{3,2,1,0:T(8,128)(2,1)S(1)} async-done(((bf16[4,2,24,128]{3,2,1,0:T(8,128)(2,1)}), bf16[4,2,24,128]{3,2,1,0:T(8,128)(2,1)S(1)}, u32[]{:S(2)}, u32[]{:S(2)}) %all-to-all-start.1) | async-done | bytes 49184 | tf_op jit(solution)/shard_map/all_to_all | solution.py:81
  75.3 1.0 %copy.71 = f32[32,24,128]{2,1,0:T(8,128)} copy(f32[32,24,128]{2,0,1:T(8,128)S(1)} %multiply_add_fusion) | data formatting | bytes 786432 | tf_op jit(solution)/shard_map/add | solution.py:121
  (46 shorter events, 3.9 us)
Async XLA Ops:
  0.0 21.1 %copy-start = (bf16[24,128,128]{2,1,0:T(8,128)(2,1)S(1)}, bf16[24,128,128]{2,1,0:T(8,128)(2,1)}, u32[]{:S(2)}) copy-start(bf16[24,128,128]{2,1,0:T(8,128)(2,1)} %param.10) | copy-start | bytes 2359300
  1.2 14.7 %collective-permute-start = (bf16[32,2,128]{2,1,0:T(2,128)(2,1)S(1)}, bf16[32,2,128]{2,1,0:T(2,128)(2,1)S(1)}, u32[]{:S(2)}, u32[]{:S(2)}) collective-permute-start(bf16[32,2,128]{2,1,0:T(2,128)(2,1)S(1)} %get-tuple-element.52), channel_id=1, source_target_pairs={{1,2},{2,1},{3,4},{4,3},{5,6},{6,5},{7,8},{8,7},{9,10},{10,9},{11,... | collective-permute-start | bytes 49160 | tf_op jit(solution)/shard_map/ppermute | solution.py:20
  9.3 6.6 %collective-permute-start.1 = (bf16[32,2,128]{2,1,0:T(2,128)(2,1)S(1)}, bf16[32,2,128]{2,1,0:T(2,128)(2,1)S(1)}, u32[]{:S(2)}, u32[]{:S(2)}) collective-permute-start(bf16[32,2,128]{2,1,0:T(2,128)(2,1)S(1)} %get-tuple-element.53), channel_id=1, source_target_pairs={{0,1},{1,0},{2,3},{3,2},{4,5},{5,4},{6,7},{7,6},{8,9},{9,8},{10,11... | collective-permute-start | bytes 49160 | tf_op jit(solution)/shard_map/ppermute | solution.py:21
  12.2 6.3 %copy-start.2 = (bf16[5,24,128,128]{3,2,1,0:T(8,128)(2,1)S(1)}, bf16[5,24,128,128]{3,2,1,0:T(8,128)(2,1)}, u32[]{:S(2)}) copy-start(bf16[5,24,128,128]{3,2,1,0:T(8,128)(2,1)} %param.9) | copy-start | bytes 11796484
  18.2 2.4 %copy-start.1 = (f32[32,24,128]{2,1,0:T(8,128)S(1)}, f32[32,24,128]{2,1,0:T(8,128)}, u32[]{:S(2)}) copy-start(f32[32,24,128]{2,1,0:T(8,128)} %param.6) | copy-start | bytes 1179652
  18.2 2.4 %copy-start.3 = (f32[32,24,128]{2,1,0:T(8,128)S(1)}, f32[32,24,128]{2,1,0:T(8,128)}, u32[]{:S(2)}) copy-start(f32[32,24,128]{2,1,0:T(8,128)} %param.7) | copy-start | bytes 1179652
  21.9 8.4 %collective-permute-start.2 = (bf16[33,2,128]{2,0,1:T(8,128)(2,1)S(1)}, bf16[33,2,128]{2,0,1:T(8,128)(2,1)S(1)}, u32[]{:S(2)}, u32[]{:S(2)}) collective-permute-start(bf16[33,2,128]{2,0,1:T(8,128)(2,1)S(1)} %get-tuple-element.19), channel_id=1, source_target_pairs={{1,2},{2,1},{3,4},{4,3},{5,6},{6,5},{7,8},{8,7},{9,10},{10,9},{11,... | collective-permute-start | bytes 50696 | tf_op jit(solution)/shard_map/ppermute | solution.py:20
  23.8 6.4 %collective-permute-start.3 = (bf16[33,2,128]{2,0,1:T(8,128)(2,1)S(1)}, bf16[33,2,128]{2,0,1:T(8,128)(2,1)S(1)}, u32[]{:S(2)}, u32[]{:S(2)}) collective-permute-start(bf16[33,2,128]{2,0,1:T(8,128)(2,1)S(1)} %get-tuple-element.18), channel_id=1, source_target_pairs={{0,1},{1,0},{2,3},{3,2},{4,5},{5,4},{6,7},{7,6},{8,9},{9,8},{10,11... | collective-permute-start | bytes 50696 | tf_op jit(solution)/shard_map/ppermute | solution.py:21
  39.5 10.4 %all-to-all-start = ((bf16[8,2,24,128]{3,2,1,0:T(8,128)(2,1)}), bf16[8,2,24,128]{3,2,1,0:T(8,128)(2,1)S(1)}, u32[]{:S(2)}, u32[]{:S(2)}) async-start(bf16[8,2,24,128]{3,2,1,0:T(8,128)(2,1)} %broadcast_in_dim.403), calls=%async_computation | async-start | bytes 196608 | tf_op jit(solution)/shard_map/all_to_all | solution.py:71
  50.6 24.3 %all-to-all-start.1 = ((bf16[4,2,24,128]{3,2,1,0:T(8,128)(2,1)}), bf16[4,2,24,128]{3,2,1,0:T(8,128)(2,1)S(1)}, u32[]{:S(2)}, u32[]{:S(2)}) async-start(bf16[4,2,24,128]{3,2,1,0:T(8,128)(2,1)} %broadcast_in_dim.406), calls=%async_computation.1 | async-start | bytes 98304 | tf_op jit(solution)/shard_map/all_to_all | solution.py:81

commit v2 on v1

v2 whole, which is shorter than its diff:
```python
import jax
import jax.numpy as jnp
from jax import lax
from jax.experimental import pallas as pl
from jax.experimental.pallas import tpu as pltpu
from jax.sharding import PartitionSpec as P

alpha_rate = 0.5
time_step = 0.5
relaxation = 0.7
GROUP = 16
EXTRA = 16
SLOTS = 5
VMEM_LIMIT = 16 * 1024 * 1024


def times_transposed(x, w):
    return lax.dot_general(x, w, (((1,), (1,)), ((), ())), preferred_element_type=jnp.float32)


def exchange(first_edge, second_edge, axis):
    count = lax.axis_size(axis)
    first, second = [], []
    for i in range(count - 1):
        (first if i & 1 else second).extend([(i, i + 1), (i + 1, i)])
    return lax.ppermute(first_edge, axis, first), lax.ppermute(second_edge, axis, second)


def is_odd():
    return (lax.axis_index("space") & 1) == 1


def fill_windows(windows, first_ref, second_ref, inside, width):
    for k in range(4):
        windows[0, 2 + k] = inside(k)
        windows[1, k] = inside(width - 4 + k)

    @pl.when(is_odd())
    def _():
        windows[0, 0:2] = second_ref[...]
        windows[1, 4:6] = first_ref[...]

    @pl.when(jnp.logical_not(is_odd()))
    def _():
        windows[0, 0:2] = first_ref[...]
        windows[1, 4:6] = second_ref[...]


def squared(state_ref, j, width, steps):
    s = state_ref[pl.ds(j, steps, stride=width), :]
    return (0.5 * s * s).astype(jnp.bfloat16)


def block_residual(j, flux, state_ref, forcing_ref, initial_ref):
    steps, lanes = flux.shape
    width = initial_ref.shape[0]
    position = lax.axis_index("tm")
    s = state_ref[pl.ds(j, steps, stride=width), :]
    f = forcing_ref[pl.ds(j, steps, stride=width), :]
    first = jnp.where(position == 0, initial_ref[pl.ds(j, 1), :], 0.0)
    row = lax.broadcasted_iota(jnp.int32, (steps, lanes), 0)
    previous = jnp.where(row == 0, jnp.broadcast_to(first, s.shape), pltpu.roll(s, 1, 0))
    residual = f - s + previous - time_step * flux
    onward = state_ref[pl.ds((steps - 1) * width + j, 1), :]
    onward = jnp.where(position == lax.axis_size("tm") - 1, 0.0, onward)
    row = lax.broadcasted_iota(jnp.int32, (EXTRA, lanes), 0)
    tail = jnp.where(row == 0, jnp.broadcast_to(onward, (EXTRA, lanes)), 0.0)
    return jnp.concatenate([residual, tail], 0)


def coupled_sum(j, at, picked, couple, blocks_ref):
    total = None
    for s in range(SLOTS):
        term = times_transposed(picked[at + couple[s, j]], blocks_ref[s, j])
        total = term if total is None else total + term
    return total


def solve_source(j, flux, state_ref, forcing_ref, initial_ref, precond_ref):
    rows = block_residual(j, flux, state_ref, forcing_ref, initial_ref)
    smooth = times_transposed(rows.astype(jnp.bfloat16), precond_ref[j])
    return 2.0 * rows - relaxation * smooth, smooth


def source_inside(couple, state_ref, forcing_ref, initial_ref, blocks_ref, precond_ref, outer_ref, smooth_ref, squares):
    width, steps, _ = squares.shape
    for j in range(width):
        squares[j] = squared(state_ref, j, width, steps)
    for j in range(2, width - 2):
        flux = coupled_sum(j, j, squares, couple, blocks_ref)
        outer, smooth = solve_source(j, flux, state_ref, forcing_ref, initial_ref, precond_ref)
        outer_ref[j - 2] = outer
        smooth_ref[j - 2] = smooth


def source_edges(couple, first_ref, second_ref, state_ref, forcing_ref, initial_ref, blocks_ref, precond_ref, outer_ref, smooth_ref, send_first, send_second, windows):
    width = initial_ref.shape[0]
    steps = windows.shape[2]
    fill_windows(windows, first_ref, second_ref, lambda k: squared(state_ref, k, width, steps), width)
    for e in range(4):
        j = e if e < 2 else width - 4 + e
        flux = coupled_sum(j, 2 + e % 2, windows.at[e // 2], couple, blocks_ref)
        outer, smooth = solve_source(j, flux, state_ref, forcing_ref, initial_ref, precond_ref)
        outer_ref[e] = outer
        smooth_ref[e] = smooth

    @pl.when(is_odd())
    def _():
        send_first[...] = smooth_ref[2:4].astype(jnp.bfloat16)
        send_second[...] = smooth_ref[0:2].astype(jnp.bfloat16)

    @pl.when(jnp.logical_not(is_odd()))
    def _():
        send_first[...] = smooth_ref[0:2].astype(jnp.bfloat16)
        send_second[...] = smooth_ref[2:4].astype(jnp.bfloat16)


def solve_block(j, coupled, outer, smooth, precond_ref, out_outer, out_inner, out_next, width):
    rows = coupled.shape[0]
    steps = rows - EXTRA
    inner = relaxation * (smooth - time_step * coupled)
    outer_high = outer.astype(jnp.bfloat16)
    outer_low = (outer - outer_high.astype(jnp.float32)).astype(jnp.bfloat16)
    inner_high = inner.astype(jnp.bfloat16)
    inner_low = (inner - inner_high.astype(jnp.float32)).astype(jnp.bfloat16)
    pieces = jnp.concatenate([outer_high, outer_low, inner_high, inner_low], 0)
    solved = times_transposed(pieces, precond_ref[j])
    outer = solved[:rows] + solved[rows : 2 * rows]
    inner = solved[2 * rows : 3 * rows] + solved[3 * rows :]
    out_outer[pl.ds(j, steps, stride=width), :] = outer[:steps]
    out_inner[pl.ds(j, steps, stride=width), :] = inner[:steps]
    out_next[pl.ds(j, 1), :] = outer[steps : steps + 1]
    out_next[pl.ds(width + j, 1), :] = inner[steps : steps + 1]


def solve_inside(couple, all_inside_ref, all_edges_ref, outer_ref, blocks_ref, precond_ref, out_outer, out_inner, out_next, rounded):
    width = rounded.shape[0]
    for k in range(2):
        rounded[k] = all_edges_ref[k].astype(jnp.bfloat16)
        rounded[width - 2 + k] = all_edges_ref[2 + k].astype(jnp.bfloat16)
    for k in range(width - 4):
        rounded[2 + k] = all_inside_ref[k].astype(jnp.bfloat16)
    out_outer[...] = jnp.zeros_like(out_outer)
    out_inner[...] = jnp.zeros_like(out_inner)
    out_next[...] = jnp.zeros_like(out_next)
    for j in range(2, width - 2):
        coupled = coupled_sum(j, j, rounded, couple, blocks_ref)
        solve_block(j, coupled, outer_ref[j - 2], all_inside_ref[j - 2], precond_ref, out_outer, out_inner, out_next, width)


def solve_edges(couple, first_ref, second_ref, all_inside_ref, all_edges_ref, outer_ref, blocks_ref, precond_ref, in_outer, in_inner, in_next, state_ref, result_ref, ends_ref, windows, my_outer, my_inner, my_next):
    width = in_next.shape[0] // 2
    steps = in_outer.shape[0] // width

    def inside(k):
        if k < 2:
            return all_edges_ref[k].astype(jnp.bfloat16)
        if k >= width - 2:
            return all_edges_ref[k - width + 4].astype(jnp.bfloat16)
        return all_inside_ref[k - 2].astype(jnp.bfloat16)

    fill_windows(windows, first_ref, second_ref, inside, width)
    my_outer[...] = in_outer[...]
    my_inner[...] = in_inner[...]
    my_next[...] = in_next[...]
    for e in range(4):
        j = e if e < 2 else width - 4 + e
        coupled = coupled_sum(j, 2 + e % 2, windows.at[e // 2], couple, blocks_ref)
        solve_block(j, coupled, outer_ref[e], all_edges_ref[e], precond_ref, my_outer, my_inner, my_next, width)
    z = jnp.zeros((width, 128), jnp.float32)
    y = jnp.zeros((width, 128), jnp.float32)
    for n in range(steps):
        rows = pl.ds(n * width, width)
        z = 0.5 * (my_inner[rows, :] + z)
        y = 0.5 * (my_outer[rows, :] + z + y)
        result_ref[rows, :] = state_ref[rows, :] + relaxation * y
    ends_outer = (y + my_next[pl.ds(0, width), :]).astype(jnp.bfloat16)
    ends_inner = (z + my_next[pl.ds(width, width), :]).astype(jnp.bfloat16)
    for k in range(ends_ref.shape[0]):
        ends_ref[k, 0] = ends_outer
        ends_ref[k, 1] = ends_inner


def finish_kernel(local_ref, carry_ref, out_ref):
    width = carry_ref.shape[1]
    steps = out_ref.shape[0] // width
    for n in range(steps):
        rows = pl.ds(n * width, width)
        scale = relaxation * 0.5 ** (n + 1)
        out_ref[rows, :] = local_ref[rows, :] + scale * (carry_ref[0] + (0.5 * (n + 1)) * carry_ref[1])


def carried(power, steps, value):
    scale = jnp.exp2(-float(steps) * power)
    return jnp.stack([scale * value[0] + scale * (0.5 * steps) * power * value[1], scale * value[1]])


def ring_carry(sent, steps):
    count = lax.axis_size("tm")
    position = lax.axis_index("tm")
    groups = count // GROUP
    members = [[g * GROUP + i for i in range(GROUP)] for g in range(groups)]
    mine = position % GROUP
    group = position // GROUP
    got = lax.all_to_all(sent, "tm", 0, 0, axis_index_groups=members, tiled=True)
    got = got.astype(jnp.float32)
    total = jnp.zeros(got.shape[1:], jnp.float32)
    before = total
    for i in range(GROUP):
        total = total + carried(jnp.float32(GROUP - 1 - i), steps, got[i])
        power = (mine - 1 - i).astype(jnp.float32)
        part = carried(jnp.maximum(power, 0.0), steps, got[i])
        before = before + jnp.where(power >= 0, part, 0.0)
    total = total.astype(jnp.bfloat16)
    into = jnp.zeros(got.shape[1:], jnp.float32)
    for m in range(1, groups + 1):
        other = total
        if m < groups:
            route = [(i, (i + m * GROUP) % count) for i in range(count)]
            other = lax.ppermute(total, "tm", route)
        wrapped = jnp.where(m > group, alpha_rate, 1.0)
        power = jnp.float32(GROUP * (m - 1))
        into = into + wrapped * carried(power, steps, other.astype(jnp.float32))
    closing = 1.0 / (1.0 - alpha_rate * 2.0 ** (-steps * count))
    return before + carried(mine.astype(jnp.float32), steps, closing * into)


def on_device(state, forcing, initial, blocks, precond, couple):
    steps, width, lanes = state.shape
    rows = steps + EXTRA
    flat = (steps * width, lanes)
    state2 = state.reshape(flat)
    forcing2 = forcing.reshape(flat)
    couple = couple.T
    f32, bf16 = jnp.float32, jnp.bfloat16

    def shaped(shape, kind=f32):
        return jax.ShapeDtypeStruct(shape, kind)

    def run(kernel, operands, results, scratch, block_rows, passes, scalars=1):
        scalar = [pl.BlockSpec(memory_space=pltpu.SMEM)] * scalars
        vector = pl.BlockSpec(memory_space=pltpu.VMEM)
        return pl.pallas_call(
            kernel,
            out_shape=results,
            in_specs=scalar + [vector] * (len(operands) - scalars),
            out_specs=[vector] * len(results),
            scratch_shapes=scratch,
            compiler_params=pltpu.CompilerParams(vmem_limit_bytes=VMEM_LIMIT),
            cost_estimate=pl.CostEstimate(
                flops=block_rows * passes * 2 * rows * lanes * lanes,
                bytes_accessed=block_rows * 6 * lanes * lanes * 2 + 1000000,
                transcendentals=0,
            ),
            name=kernel.__name__,
        )(*operands)

    low_edge = (0.5 * state[:, :2] * state[:, :2]).astype(bf16).transpose(1, 0, 2)
    high_edge = (0.5 * state[:, -2:] * state[:, -2:]).astype(bf16).transpose(1, 0, 2)
    odd = is_odd()
    first, second = exchange(
        jnp.where(odd, high_edge, low_edge), jnp.where(odd, low_edge, high_edge), "space"
    )

    outer_in, smooth_in = run(
        source_inside,
        (couple, state2, forcing2, initial, blocks, precond),
        [shaped((width - 4, rows, lanes))] * 2,
        [pltpu.VMEM((width, steps, lanes), bf16)],
        width - 4,
        6,
    )
    outer_ed, smooth_ed, send_first, send_second = run(
        source_edges,
        (couple, first, second, state2, forcing2, initial, blocks, precond),
        [shaped((4, rows, lanes))] * 2 + [shaped((2, rows, lanes), bf16)] * 2,
        [pltpu.VMEM((2, 6, steps, lanes), bf16)],
        4,
        6,
    )
    first, second = exchange(send_first, send_second, "space")
    out_outer, out_inner, out_next = run(
        solve_inside,
        (couple, smooth_in, smooth_ed, outer_in, blocks, precond),
        [shaped(flat), shaped(flat), shaped((2 * width, lanes))],
        [pltpu.VMEM((width, rows, lanes), bf16)],
        width - 4,
        9,
    )
    local, ends = run(
        solve_edges,
        (couple, first, second, smooth_in, smooth_ed, outer_ed, blocks, precond, out_outer, out_inner, out_next, state2),
        [shaped(flat), shaped((GROUP, 2, width, lanes), bf16)],
        [
            pltpu.VMEM((2, 6, rows, lanes), bf16),
            pltpu.VMEM(flat, f32),
            pltpu.VMEM(flat, f32),
            pltpu.VMEM((2 * width, lanes), f32),
        ],
        4,
        9,
    )
    carry = ring_carry(ends, steps)
    (out,) = run(finish_kernel, (local, carry), [shaped(flat)], [], 1, 1, 0)
    return out.reshape(state.shape)


def solution(mesh):
    placed = (
        P("tm", "space", None),
        P("tm", "space", None),
        P("space", None),
        P(None, "space", None, None),
        P("space", None, None),
        P("space", None),
    )
    return jax.shard_map(
        on_device, mesh=mesh, in_specs=placed, out_specs=P("tm", "space", None), check_vma=False
    )
```

time: 77.1 us -> 71.3 us (0.925)
  the two profiles are of different devices: /device:TPU:6 before, /device:TPU:1 now
where the time goes in v2:
time: 71.3 us; the launch traced here: 70.8 us
  starting transfers between devices  32.8 us (46%)
  Pallas kernels  18.3 us (26%)
  waiting for transfers between devices  10.8 us (15%)
  local copies, waits for them, and re-layouts  7.63 us (11%)
  between operations  1.04 us (1%)
    pallas_call x5, Pallas kernels, run(): pl.pallas_call(kernel, out_shape=results, in_specs=scalar + [vector] * (l...  18.3 us
    ppermute x2, starting transfers between devices, exchange(): lax.ppermute(second_edge, axis, second)  13.4 us
    all_to_all x1, waiting for transfers between devices, ring_carry(): lax.all_to_all(sent, 'tm', 0, 0, axis_index_groups=members, tiled=True)  9.42 us
    ppermute x1, starting transfers between devices, ring_carry(): other = lax.ppermute(total, 'tm', route)  9.39 us
    all_to_all x1, starting transfers between devices, ring_carry(): lax.all_to_all(sent, 'tm', 0, 0, axis_index_groups=members, tiled=True)  8.63 us
    unnamed x18, local copies, waits for them, and re-layouts  6.64 us
  transfers between devices with their start and end apart: 6, of which 2 were waited for; matrix products, arithmetic and copies ran while one was open for 0% of the time, Pallas kernels for 18%

profile of v2, /device:TPU:1, one launch (start us, length us, event | category | flops | bytes accessed | tf_op | source)
XLA Modules:
  0.0 70.8 jit_solution(5199835495259046451)
XLA Ops:
  0.0 1.0 %fusion.38 = (f32[32,2,128]{2,1,0:T(2,128)S(1)}, f32[32,2,128]{2,1,0:T(2,128)S(1)}) fusion(f32[32,24,128]{2,1,0:T(8,128)} %param.6), kind=kLoop, calls=%fused_computation.130 | loop fusion | bytes 131072 | tf_op jit(solution)/shard_map/slice | solution.py:259
  1.0 0.7 collective-permute-start
  1.7 8.2 %collective-permute-start.1 = (bf16[2,32,128]{2,1,0:T(8,128)(2,1)S(1)}, bf16[2,32,128]{2,1,0:T(8,128)(2,1)S(1)}, u32[]{:S(2)}, u32[]{:S(2)}) collective-permute-start(bf16[2,32,128]{2,1,0:T(8,128)(2,1)S(1)} %get-tuple-element.95), channel_id=1, source_target_pairs={{0,1},{1,0},{2,3},{3,2},{4,5},{5,4},{6,7},{7,6},{8,9},{9,8},{10,11... | collective-permute-start | bytes 49160 | tf_op jit(solution)/shard_map/ppermute | solution.py:26
  9.9 0.0 copy-start
  9.9 2.1 %copy-done = bf16[5,24,128,128]{3,2,1,0:T(8,128)(2,1)S(1)} copy-done((bf16[5,24,128,128]{3,2,1,0:T(8,128)(2,1)S(1)}, bf16[5,24,128,128]{3,2,1,0:T(8,128)(2,1)}, u32[]{:S(2)}) %copy-start) | copy-done | bytes 3932184
  12.0 0.0 copy-start.2
  12.0 1.1 %copy-done.2 = bf16[24,128,128]{2,1,0:T(8,128)(2,1)S(1)} copy-done((bf16[24,128,128]{2,1,0:T(8,128)(2,1)S(1)}, bf16[24,128,128]{2,1,0:T(8,128)(2,1)}, u32[]{:S(2)}) %copy-start.2) | copy-done | bytes 786456
  13.1 0.0 copy-start.4
  13.1 1.0 %copy-done.4 = f32[32,24,128]{2,1,0:T(8,128)S(1)} copy-done((f32[32,24,128]{2,1,0:T(8,128)S(1)}, f32[32,24,128]{2,1,0:T(8,128)}, u32[]{:S(2)}) %copy-start.4) | copy-done | bytes 393240
  14.1 1.0 %copy-done.6 = f32[32,24,128]{2,1,0:T(8,128)S(1)} copy-done((f32[32,24,128]{2,1,0:T(8,128)S(1)}, f32[32,24,128]{2,1,0:T(8,128)}, u32[]{:S(2)}) %copy-start.6) | copy-done | bytes 393240
  15.1 0.7 copy-done.7
  15.8 0.7 copy-done.8
  16.5 6.5 %source_inside.1 = (f32[20,48,128]{2,1,0:T(8,128)S(1)}, f32[20,48,128]{2,1,0:T(8,128)S(1)}) custom-call(s32[5,24]{1,0:T(8,128)S(1)} %bitcast.169, f32[768,128]{1,0:T(8,128)S(1)} %bitcast.164, f32[768,128]{1,0:T(8,128)S(1)} %bitcast.167, f32[24,128]{1,0:T(8,128)S(1)} %copy-done.8, bf16[5,24,128,128]{3,2,1,0:T(8,128)(2,1)S(1)} %copy-done, ...), custom_call_target="tpu_custom_call" | custom-call | flops 188743680 | bytes 4932160 | tf_op jit(solution)/shard_map/source_inside/pallas_call | solution.py:243
  23.0 0.0 copy-start.3
  23.1 0.0 collective-permute-done.first_ref
  23.1 0.0 collective-permute-done.1.second_ref
  23.1 0.0 copy-done.1
  23.1 0.0 copy-done.5
  23.1 1.9 %source_edges.1 = (f32[4,48,128]{2,1,0:T(8,128)S(1)}, f32[4,48,128]{2,1,0:T(8,128)S(1)}, bf16[2,48,128]{2,1,0:T(8,128)(2,1)S(1)}, bf16[2,48,128]{2,1,0:T(8,128)(2,1)S(1)}) custom-call(s32[5,24]{1,0:T(8,128)S(1)} %bitcast.170, bf16[2,32,128]{2,1,0:T(8,128)(2,1)S(1)} %collective-permute-done.first_ref, ...), custom_call_target="tpu_custom_call" | custom-call | flops 37748736 | bytes 1786432 | tf_op jit(solution)/shard_map/source_edges/pallas_call | solution.py:243
  25.0 0.7 collective-permute-start.2
  25.7 5.3 %collective-permute-start.3 = (bf16[2,48,128]{2,1,0:T(8,128)(2,1)S(1)}, bf16[2,48,128]{2,1,0:T(8,128)(2,1)S(1)}, u32[]{:S(2)}, u32[]{:S(2)}) collective-permute-start(bf16[2,48,128]{2,1,0:T(8,128)(2,1)S(1)} %get-tuple-element.17), channel_id=1, source_target_pairs={{0,1},{1,0},{2,3},{3,2},{4,5},{5,4},{6,7},{7,6},{8,9},{9,8},{10,11... | collective-permute-start | bytes 73736 | tf_op jit(solution)/shard_map/ppermute | solution.py:26
  31.0 0.0 copy-done.3
  31.0 6.4 %solve_inside.1 = (f32[768,128]{1,0:T(8,128)S(1)}, f32[768,128]{1,0:T(8,128)S(1)}, f32[48,128]{1,0:T(8,128)S(1)}) custom-call(s32[5,24]{1,0:T(8,128)S(1)} %bitcast.171, f32[20,48,128]{2,1,0:T(8,128)S(1)} %get-tuple-element.18.all_inside_ref, f32[4,48,128]{2,1,0:T(8,128)S(1)} %get-tuple-element.19.all_edges_ref, ...), custom_call_target="tpu_custom_call" | custom-call | flops 283115520 | bytes 4932160 | tf_op jit(solution)/shard_map/solve_inside/pallas_call | solution.py:243
  37.3 0.0 collective-permute-done.2.first_ref
  37.4 0.0 collective-permute-done.3.second_ref
  37.4 2.6 %solve_edges.1 = (f32[768,128]{1,0:T(8,128)S(1)}, bf16[16,2,24,128]{3,2,1,0:T(8,128)(2,1)}) custom-call(s32[5,24]{1,0:T(8,128)S(1)} %bitcast.172, bf16[2,48,128]{2,1,0:T(8,128)(2,1)S(1)} %collective-permute-done.2.first_ref, bf16[2,48,128]{2,1,0:T(8,128)(2,1)S(1)} %collective-permute-done.3.second_ref, f32[20,48,128]{2,1,0:T(8,128)S(1)} %get-tuple-element.18.all_inside_ref, ...), custom_call_target="tpu_custom_call" | custom-call | flops 56623104 | bytes 1786432 | tf_op jit(solution)/shard_map/solve_edges/pallas_call | solution.py:243
  40.0 8.6 %all-to-all-start = ((bf16[16,2,24,128]{3,2,1,0:T(8,128)(2,1)}), bf16[16,2,24,128]{3,2,1,0:T(8,128)(2,1)S(1)}, u32[]{:S(2)}, u32[]{:S(2)}) async-start(bf16[16,2,24,128]{3,2,1,0:T(8,128)(2,1)} %get-tuple-element.26), calls=%async_computation | async-start | bytes 393216 | tf_op jit(solution)/shard_map/all_to_all | solution.py:205
  49.4 9.4 %all-to-all-done = bf16[16,2,24,128]{3,2,1,0:T(8,128)(2,1)S(1)} async-done(((bf16[16,2,24,128]{3,2,1,0:T(8,128)(2,1)}), bf16[16,2,24,128]{3,2,1,0:T(8,128)(2,1)S(1)}, u32[]{:S(2)}, u32[]{:S(2)}) %all-to-all-start) | async-done | bytes 196640 | tf_op jit(solution)/shard_map/all_to_all | solution.py:205
  59.0 9.4 %collective-permute-start.4 = (bf16[2,24,128]{2,1,0:T(8,128)(2,1)S(1)}, bf16[2,24,128]{2,1,0:T(8,128)(2,1)S(1)}, u32[]{:S(2)}, u32[]{:S(2)}) collective-permute-start(bf16[2,24,128]{2,1,0:T(8,128)(2,1)S(1)} %get-tuple-element.28), channel_id=1, source_target_pairs={{0,256},{16,272},{32,288},{48,304},{64,320},{80,336},{96,352},{112... | collective-permute-start | bytes 36872 | tf_op jit(solution)/shard_map/ppermute | solution.py:220
  68.5 1.3 %collective-permute-done.4 = bf16[2,24,128]{2,1,0:T(8,128)(2,1)S(1)} collective-permute-done((bf16[2,24,128]{2,1,0:T(8,128)(2,1)S(1)}, bf16[2,24,128]{2,1,0:T(8,128)(2,1)S(1)}, u32[]{:S(2)}, u32[]{:S(2)}) %collective-permute-start.4) | collective-permute-done | bytes 12320 | tf_op jit(solution)/shard_map/ppermute | solution.py:220
  69.9 0.1 fusion.17.carry_ref
  70.0 0.8 %finish_kernel.1 = f32[768,128]{1,0:T(8,128)} custom-call(f32[768,128]{1,0:T(8,128)S(1)} %get-tuple-element.25.local_ref, f32[2,24,128]{2,1,0:T(8,128)S(1)} %fusion.17.carry_ref), custom_call_target="tpu_custom_call" | custom-call | flops 1572864 | bytes 1196608 | tf_op jit(solution)/shard_map/finish_kernel/pallas_call | solution.py:243
  (22 shorter events, 0.3 us)
Async XLA Ops:
  1.0 22.0 %collective-permute-start = (bf16[2,32,128]{2,1,0:T(8,128)(2,1)S(1)}, bf16[2,32,128]{2,1,0:T(8,128)(2,1)S(1)}, u32[]{:S(2)}, u32[]{:S(2)}) collective-permute-start(bf16[2,32,128]{2,1,0:T(8,128)(2,1)S(1)} %get-tuple-element.96), channel_id=1, source_target_pairs={{1,2},{2,1},{3,4},{4,3},{5,6},{6,5},{7,8},{8,7},{9,10},{10,9},{11,... | collective-permute-start | bytes 49160 | tf_op jit(solution)/shard_map/ppermute | solution.py:26
  1.7 21.4 %collective-permute-start.1 = (bf16[2,32,128]{2,1,0:T(8,128)(2,1)S(1)}, bf16[2,32,128]{2,1,0:T(8,128)(2,1)S(1)}, u32[]{:S(2)}, u32[]{:S(2)}) collective-permute-start(bf16[2,32,128]{2,1,0:T(8,128)(2,1)S(1)} %get-tuple-element.95), channel_id=1, source_target_pairs={{0,1},{1,0},{2,3},{3,2},{4,5},{5,4},{6,7},{7,6},{8,9},{9,8},{10,11... | collective-permute-start | bytes 49160 | tf_op jit(solution)/shard_map/ppermute | solution.py:26
  9.9 2.1 %copy-start = (bf16[5,24,128,128]{3,2,1,0:T(8,128)(2,1)S(1)}, bf16[5,24,128,128]{3,2,1,0:T(8,128)(2,1)}, u32[]{:S(2)}) copy-start(bf16[5,24,128,128]{3,2,1,0:T(8,128)(2,1)} %blocks_ref.7) | copy-start | bytes 11796484
  12.0 1.1 %copy-start.2 = (bf16[24,128,128]{2,1,0:T(8,128)(2,1)S(1)}, bf16[24,128,128]{2,1,0:T(8,128)(2,1)}, u32[]{:S(2)}) copy-start(bf16[24,128,128]{2,1,0:T(8,128)(2,1)} %precond_ref.7) | copy-start | bytes 2359300
  13.1 1.0 %copy-start.4 = (f32[32,24,128]{2,1,0:T(8,128)S(1)}, f32[32,24,128]{2,1,0:T(8,128)}, u32[]{:S(2)}) copy-start(f32[32,24,128]{2,1,0:T(8,128)} %param.6) | copy-start | bytes 1179652
  14.1 1.0 %copy-start.6 = (f32[32,24,128]{2,1,0:T(8,128)S(1)}, f32[32,24,128]{2,1,0:T(8,128)}, u32[]{:S(2)}) copy-start(f32[32,24,128]{2,1,0:T(8,128)} %param.7) | copy-start | bytes 1179652
  15.1 0.7 copy-start.7
  15.8 0.7 copy-start.8
  16.5 6.6 %copy-start.1 = (bf16[5,24,128,128]{3,2,1,0:T(8,128)(2,1)S(1)}, bf16[5,24,128,128]{3,2,1,0:T(8,128)(2,1)}, u32[]{:S(2)}) copy-start(bf16[5,24,128,128]{3,2,1,0:T(8,128)(2,1)} %blocks_ref.7) | copy-start | bytes 11796484
  16.5 6.6 %copy-start.5 = (f32[32,24,128]{2,1,0:T(8,128)S(1)}, f32[32,24,128]{2,1,0:T(8,128)}, u32[]{:S(2)}) copy-start(f32[32,24,128]{2,1,0:T(8,128)} %param.6) | copy-start | bytes 1179652
  23.0 7.9 %copy-start.3 = (bf16[24,128,128]{2,1,0:T(8,128)(2,1)S(1)}, bf16[24,128,128]{2,1,0:T(8,128)(2,1)}, u32[]{:S(2)}) copy-start(bf16[24,128,128]{2,1,0:T(8,128)(2,1)} %precond_ref.7) | copy-start | bytes 2359300
  25.0 12.3 %collective-permute-start.2 = (bf16[2,48,128]{2,1,0:T(8,128)(2,1)S(1)}, bf16[2,48,128]{2,1,0:T(8,128)(2,1)S(1)}, u32[]{:S(2)}, u32[]{:S(2)}) collective-permute-start(bf16[2,48,128]{2,1,0:T(8,128)(2,1)S(1)} %get-tuple-element.16), channel_id=1, source_target_pairs={{1,2},{2,1},{3,4},{4,3},{5,6},{6,5},{7,8},{8,7},{9,10},{10,9},{11,... | collective-permute-start | bytes 73736 | tf_op jit(solution)/shard_map/ppermute | solution.py:26
  25.7 11.7 %collective-permute-start.3 = (bf16[2,48,128]{2,1,0:T(8,128)(2,1)S(1)}, bf16[2,48,128]{2,1,0:T(8,128)(2,1)S(1)}, u32[]{:S(2)}, u32[]{:S(2)}) collective-permute-start(bf16[2,48,128]{2,1,0:T(8,128)(2,1)S(1)} %get-tuple-element.17), channel_id=1, source_target_pairs={{0,1},{1,0},{2,3},{3,2},{4,5},{5,4},{6,7},{7,6},{8,9},{9,8},{10,11... | collective-permute-start | bytes 73736 | tf_op jit(solution)/shard_map/ppermute | solution.py:26
  40.0 18.8 %all-to-all-start = ((bf16[16,2,24,128]{3,2,1,0:T(8,128)(2,1)}), bf16[16,2,24,128]{3,2,1,0:T(8,128)(2,1)S(1)}, u32[]{:S(2)}, u32[]{:S(2)}) async-start(bf16[16,2,24,128]{3,2,1,0:T(8,128)(2,1)} %get-tuple-element.26), calls=%async_computation | async-start | bytes 393216 | tf_op jit(solution)/shard_map/all_to_all | solution.py:205
  59.0 10.8 %collective-permute-start.4 = (bf16[2,24,128]{2,1,0:T(8,128)(2,1)S(1)}, bf16[2,24,128]{2,1,0:T(8,128)(2,1)S(1)}, u32[]{:S(2)}, u32[]{:S(2)}) collective-permute-start(bf16[2,24,128]{2,1,0:T(8,128)(2,1)S(1)} %get-tuple-element.28), channel_id=1, source_target_pairs={{0,256},{16,272},{32,288},{48,304},{64,320},{80,336},{96,352},{112... | collective-permute-start | bytes 36872 | tf_op jit(solution)/shard_map/ppermute | solution.py:220

commit v3 on v2

--- a/solution.py
+++ b/solution.py
@@ -11,6 +11,7 @@
 GROUP = 16
 EXTRA = 16
 SLOTS = 5
+PREFETCH_ROWS = 400
 VMEM_LIMIT = 16 * 1024 * 1024
 
 
@@ -69,17 +70,32 @@
 
 
 def coupled_sum(j, at, picked, couple, blocks_ref):
-    total = None
-    for s in range(SLOTS):
-        term = times_transposed(picked[at + couple[s, j]], blocks_ref[s, j])
-        total = term if total is None else total + term
-    return total
+    rows = jnp.concatenate([picked[at + couple[s, j]] for s in range(SLOTS)], 1)
+    weights = jnp.concatenate([blocks_ref[s, j] for s in range(SLOTS)], 1)
+    return times_transposed(rows, weights)
 
 
 def solve_source(j, flux, state_ref, forcing_ref, initial_ref, precond_ref):
     rows = block_residual(j, flux, state_ref, forcing_ref, initial_ref)
     smooth = times_transposed(rows.astype(jnp.bfloat16), precond_ref[j])
     return 2.0 * rows - relaxation * smooth, smooth
+
+
+def edge_squares(state_ref, send_first, send_second):
+    _, steps, _ = send_first.shape
+    width = state_ref.shape[0] // steps
+
+    @pl.when(is_odd())
+    def _():
+        for k in range(2):
+            send_first[k] = squared(state_ref, width - 2 + k, width, steps)
+            send_second[k] = squared(state_ref, k, width, steps)
+
+    @pl.when(jnp.logical_not(is_odd()))
+    def _():
+        for k in range(2):
+            send_first[k] = squared(state_ref, k, width, steps)
+            send_second[k] = squared(state_ref, width - 2 + k, width, steps)
 
 
 def source_inside(couple, state_ref, forcing_ref, initial_ref, blocks_ref, precond_ref, outer_ref, smooth_ref, squares):
@@ -255,12 +271,10 @@
             name=kernel.__name__,
         )(*operands)
 
-    low_edge = (0.5 * state[:, :2] * state[:, :2]).astype(bf16).transpose(1, 0, 2)
-    high_edge = (0.5 * state[:, -2:] * state[:, -2:]).astype(bf16).transpose(1, 0, 2)
-    odd = is_odd()
-    first, second = exchange(
-        jnp.where(odd, high_edge, low_edge), jnp.where(odd, low_edge, high_edge), "space"
-    )
+    send_first, send_second = run(
+        edge_squares, (state2,), [shaped((2, steps, lanes), bf16)] * 2, [], PREFETCH_ROWS, 6, 0
+    )
+    first, second = exchange(send_first, send_second, "space")
 
     outer_in, smooth_in = run(
         source_inside,

time: 71.3 us -> 60.1 us (0.84)
  local copies, waits for them, and re-layouts: 7.63 us -> 1.02 us
  Pallas kernels: 18.3 us -> 13.5 us
    unnamed x18 -> x14, local copies, waits for them, and re-layouts: 6.64 us -> 1.02 us
    pallas_call x5 -> x6, Pallas kernels: 18.3 us -> 13.5 us  [run(): pl.pallas_call(kernel, out_shape=results, in_specs=scalar + [vector] * (l...]
    slice x1 -> x0, local copies, waits for them, and re-layouts: 0.99 us -> none  [on_device(): state[:, -2:]]
  transfers between devices with their start and end apart: 6 -> 6, of which waited for: 2 -> 2; matrix products, arithmetic and copies ran while one was open for 0% -> 0% of each run, Pallas kernels for 18% -> 15%
where the time goes in v3:
time: 60.1 us; the launch traced here: 59.8 us
  starting transfers between devices  33.1 us (55%)
  Pallas kernels  13.5 us (22%)
  waiting for transfers between devices  10.7 us (18%)
  between operations  1.06 us (2%)
  local copies, waits for them, and re-layouts  1.02 us (2%)
    ppermute x2, starting transfers between devices, exchange(): lax.ppermute(second_edge, axis, second)  13.5 us
    pallas_call x6, Pallas kernels, run(): pl.pallas_call(kernel, out_shape=results, in_specs=scalar + [vector] * (l...  13.5 us
    all_to_all x1, waiting for transfers between devices, ring_carry(): lax.all_to_all(sent, 'tm', 0, 0, axis_index_groups=members, tiled=True)  9.42 us
    ppermute x1, starting transfers between devices, ring_carry(): other = lax.ppermute(total, 'tm', route)  9.38 us
    all_to_all x1, starting transfers between devices, ring_carry(): lax.all_to_all(sent, 'tm', 0, 0, axis_index_groups=members, tiled=True)  8.63 us
    ppermute x2, starting transfers between devices, exchange(): lax.ppermute(first_edge, axis, first)  1.59 us
    ppermute x1, waiting for transfers between devices, ring_carry(): other = lax.ppermute(total, 'tm', route)  1.31 us
  transfers between devices with their start and end apart: 6, of which 2 were waited for; matrix products, arithmetic and copies ran while one was open for 0% of the time, Pallas kernels for 15%

profile of v3, /device:TPU:1, one launch (start us, length us, event | category | flops | bytes accessed | tf_op | source)
XLA Modules:
  0.0 59.8 jit_solution(10762151477103144026)
XLA Ops:
  0.0 0.0 copy-start.2
  0.0 1.0 %copy-done.2 = f32[32,24,128]{2,1,0:T(8,128)S(1)} copy-done((f32[32,24,128]{2,1,0:T(8,128)S(1)}, f32[32,24,128]{2,1,0:T(8,128)}, u32[]{:S(2)}) %copy-start.2) | copy-done | bytes 393240
  1.0 0.0 copy-start
  1.0 0.0 copy-start.1
  1.0 0.0 copy-start.4
  1.0 0.0 copy-start.5
  1.0 0.0 copy-start.6
  1.1 0.8 %collective-permute-start = (bf16[2,32,128]{2,1,0:T(8,128)(2,1)S(1)}, bf16[2,32,128]{2,1,0:T(8,128)(2,1)S(1)}, u32[]{:S(2)}, u32[]{:S(2)}) collective-permute-start(bf16[2,32,128]{2,1,0:T(8,128)(2,1)S(1)} %get-tuple-element.18), channel_id=1, source_target_pairs={{1,2},{2,1},{3,4},{4,3},{5,6},{6,5},{7,8},{8,7},{9,10},{10,9},{11,... | collective-permute-start | bytes 49160 | tf_op jit(solution)/shard_map/ppermute | solution.py:27
  1.9 8.3 %collective-permute-start.1 = (bf16[2,32,128]{2,1,0:T(8,128)(2,1)S(1)}, bf16[2,32,128]{2,1,0:T(8,128)(2,1)S(1)}, u32[]{:S(2)}, u32[]{:S(2)}) collective-permute-start(bf16[2,32,128]{2,1,0:T(8,128)(2,1)S(1)} %get-tuple-element.19), channel_id=1, source_target_pairs={{0,1},{1,0},{2,3},{3,2},{4,5},{5,4},{6,7},{7,6},{8,9},{9,8},{10,11... | collective-permute-start | bytes 49160 | tf_op jit(solution)/shard_map/ppermute | solution.py:27
  10.2 0.0 copy-done
  10.2 0.0 copy-done.1
  10.2 0.0 copy-done.4
  10.2 0.0 copy-done.5
  10.2 0.0 copy-done.6
  10.2 3.9 %source_inside.1 = (f32[20,48,128]{2,1,0:T(8,128)S(1)}, f32[20,48,128]{2,1,0:T(8,128)S(1)}) custom-call(s32[5,24]{1,0:T(8,128)S(1)} %bitcast.166, f32[768,128]{1,0:T(8,128)S(1)} %bitcast.161, f32[768,128]{1,0:T(8,128)S(1)} %bitcast.164, f32[24,128]{1,0:T(8,128)S(1)} %copy-done.6, bf16[5,24,128,128]{3,2,1,0:T(8,128)(2,1)S(1)} %copy-done, ...), custom_call_target="tpu_custom_call" | custom-call | flops 188743680 | bytes 4932160 | tf_op jit(solution)/shard_map/source_inside/pallas_call | solution.py:259
  14.2 0.0 collective-permute-done.first_ref
  14.2 0.0 collective-permute-done.1.second_ref
  14.2 1.4 %source_edges.1 = (f32[4,48,128]{2,1,0:T(8,128)S(1)}, f32[4,48,128]{2,1,0:T(8,128)S(1)}, bf16[2,48,128]{2,1,0:T(8,128)(2,1)S(1)}, bf16[2,48,128]{2,1,0:T(8,128)(2,1)S(1)}) custom-call(s32[5,24]{1,0:T(8,128)S(1)} %bitcast.167, bf16[2,32,128]{2,1,0:T(8,128)(2,1)S(1)} %collective-permute-done.first_ref, ...), custom_call_target="tpu_custom_call" | custom-call | flops 37748736 | bytes 1786432 | tf_op jit(solution)/shard_map/source_edges/pallas_call | solution.py:259
  15.6 0.0 copy-start.3
  15.6 0.8 %collective-permute-start.2 = (bf16[2,48,128]{2,1,0:T(8,128)(2,1)S(1)}, bf16[2,48,128]{2,1,0:T(8,128)(2,1)S(1)}, u32[]{:S(2)}, u32[]{:S(2)}) collective-permute-start(bf16[2,48,128]{2,1,0:T(8,128)(2,1)S(1)} %get-tuple-element.20), channel_id=1, source_target_pairs={{1,2},{2,1},{3,4},{4,3},{5,6},{6,5},{7,8},{8,7},{9,10},{10,9},{11,... | collective-permute-start | bytes 73736 | tf_op jit(solution)/shard_map/ppermute | solution.py:27
  16.4 5.3 %collective-permute-start.3 = (bf16[2,48,128]{2,1,0:T(8,128)(2,1)S(1)}, bf16[2,48,128]{2,1,0:T(8,128)(2,1)S(1)}, u32[]{:S(2)}, u32[]{:S(2)}) collective-permute-start(bf16[2,48,128]{2,1,0:T(8,128)(2,1)S(1)} %get-tuple-element.21), channel_id=1, source_target_pairs={{0,1},{1,0},{2,3},{3,2},{4,5},{5,4},{6,7},{7,6},{8,9},{9,8},{10,11... | collective-permute-start | bytes 73736 | tf_op jit(solution)/shard_map/ppermute | solution.py:27
  21.7 4.9 %solve_inside.1 = (f32[768,128]{1,0:T(8,128)S(1)}, f32[768,128]{1,0:T(8,128)S(1)}, f32[48,128]{1,0:T(8,128)S(1)}) custom-call(s32[5,24]{1,0:T(8,128)S(1)} %bitcast.168, f32[20,48,128]{2,1,0:T(8,128)S(1)} %get-tuple-element.22.all_inside_ref, f32[4,48,128]{2,1,0:T(8,128)S(1)} %get-tuple-element.23.all_edges_ref, ...), custom_call_target="tpu_custom_call" | custom-call | flops 283115520 | bytes 4932160 | tf_op jit(solution)/shard_map/solve_inside/pallas_call | solution.py:259
  26.6 0.0 collective-permute-done.2.first_ref
  26.6 0.0 collective-permute-done.3.second_ref
  26.6 0.0 copy-done.3
  26.6 2.4 %solve_edges.1 = (f32[768,128]{1,0:T(8,128)S(1)}, bf16[16,2,24,128]{3,2,1,0:T(8,128)(2,1)}) custom-call(s32[5,24]{1,0:T(8,128)S(1)} %bitcast.169, bf16[2,48,128]{2,1,0:T(8,128)(2,1)S(1)} %collective-permute-done.2.first_ref, bf16[2,48,128]{2,1,0:T(8,128)(2,1)S(1)} %collective-permute-done.3.second_ref, f32[20,48,128]{2,1,0:T(8,128)S(1)} %get-tuple-element.22.all_inside_ref, ...), custom_call_target="tpu_custom_call" | custom-call | flops 56623104 | bytes 1786432 | tf_op jit(solution)/shard_map/solve_edges/pallas_call | solution.py:259
  29.0 8.6 %all-to-all-start = ((bf16[16,2,24,128]{3,2,1,0:T(8,128)(2,1)}), bf16[16,2,24,128]{3,2,1,0:T(8,128)(2,1)S(1)}, u32[]{:S(2)}, u32[]{:S(2)}) async-start(bf16[16,2,24,128]{3,2,1,0:T(8,128)(2,1)} %get-tuple-element.30), calls=%async_computation | async-start | bytes 393216 | tf_op jit(solution)/shard_map/all_to_all | solution.py:221
  38.4 9.4 %all-to-all-done = bf16[16,2,24,128]{3,2,1,0:T(8,128)(2,1)S(1)} async-done(((bf16[16,2,24,128]{3,2,1,0:T(8,128)(2,1)}), bf16[16,2,24,128]{3,2,1,0:T(8,128)(2,1)S(1)}, u32[]{:S(2)}, u32[]{:S(2)}) %all-to-all-start) | async-done | bytes 196640 | tf_op jit(solution)/shard_map/all_to_all | solution.py:221
  48.0 9.4 %collective-permute-start.4 = (bf16[2,24,128]{2,1,0:T(8,128)(2,1)S(1)}, bf16[2,24,128]{2,1,0:T(8,128)(2,1)S(1)}, u32[]{:S(2)}, u32[]{:S(2)}) collective-permute-start(bf16[2,24,128]{2,1,0:T(8,128)(2,1)S(1)} %get-tuple-element.32), channel_id=1, source_target_pairs={{0,256},{16,272},{32,288},{48,304},{64,320},{80,336},{96,352},{112... | collective-permute-start | bytes 36872 | tf_op jit(solution)/shard_map/ppermute | solution.py:236
  57.5 1.3 %collective-permute-done.4 = bf16[2,24,128]{2,1,0:T(8,128)(2,1)S(1)} collective-permute-done((bf16[2,24,128]{2,1,0:T(8,128)(2,1)S(1)}, bf16[2,24,128]{2,1,0:T(8,128)(2,1)S(1)}, u32[]{:S(2)}, u32[]{:S(2)}) %collective-permute-start.4) | collective-permute-done | bytes 12320 | tf_op jit(solution)/shard_map/ppermute | solution.py:236
  58.9 0.1 fusion.15.carry_ref
  59.0 0.8 %finish_kernel.1 = f32[768,128]{1,0:T(8,128)} custom-call(f32[768,128]{1,0:T(8,128)S(1)} %get-tuple-element.29.local_ref, f32[2,24,128]{2,1,0:T(8,128)S(1)} %fusion.15.carry_ref), custom_call_target="tpu_custom_call" | custom-call | flops 1572864 | bytes 1196608 | tf_op jit(solution)/shard_map/finish_kernel/pallas_call | solution.py:259
  (17 shorter events, 0.3 us)
Async XLA Ops:
  0.0 1.0 %copy-start.2 = (f32[32,24,128]{2,1,0:T(8,128)S(1)}, f32[32,24,128]{2,1,0:T(8,128)}, u32[]{:S(2)}) copy-start(f32[32,24,128]{2,1,0:T(8,128)} %param.6) | copy-start | bytes 1179652
  1.0 9.2 %copy-start = (bf16[5,24,128,128]{3,2,1,0:T(8,128)(2,1)S(1)}, bf16[5,24,128,128]{3,2,1,0:T(8,128)(2,1)}, u32[]{:S(2)}) copy-start(bf16[5,24,128,128]{3,2,1,0:T(8,128)(2,1)} %blocks_ref.7) | copy-start | bytes 11796484
  1.0 9.2 %copy-start.1 = (bf16[24,128,128]{2,1,0:T(8,128)(2,1)S(1)}, bf16[24,128,128]{2,1,0:T(8,128)(2,1)}, u32[]{:S(2)}) copy-start(bf16[24,128,128]{2,1,0:T(8,128)(2,1)} %precond_ref.7) | copy-start | bytes 2359300
  1.0 9.2 %copy-start.4 = (f32[32,24,128]{2,1,0:T(8,128)S(1)}, f32[32,24,128]{2,1,0:T(8,128)}, u32[]{:S(2)}) copy-start(f32[32,24,128]{2,1,0:T(8,128)} %param.7) | copy-start | bytes 1179652
  1.0 9.2 %copy-start.5 = (s32[24,5]{0,1:T(8,128)S(1)}, s32[24,5]{0,1:T(8,128)}, u32[]{:S(2)}) copy-start(s32[24,5]{0,1:T(8,128)} %param.11) | copy-start | bytes 1444
  1.0 9.2 %copy-start.6 = (f32[24,128]{1,0:T(8,128)S(1)}, f32[24,128]{1,0:T(8,128)}, u32[]{:S(2)}) copy-start(f32[24,128]{1,0:T(8,128)} %initial_ref.3) | copy-start | bytes 36868
  1.1 13.1 %collective-permute-start = (bf16[2,32,128]{2,1,0:T(8,128)(2,1)S(1)}, bf16[2,32,128]{2,1,0:T(8,128)(2,1)S(1)}, u32[]{:S(2)}, u32[]{:S(2)}) collective-permute-start(bf16[2,32,128]{2,1,0:T(8,128)(2,1)S(1)} %get-tuple-element.18), channel_id=1, source_target_pairs={{1,2},{2,1},{3,4},{4,3},{5,6},{6,5},{7,8},{8,7},{9,10},{10,9},{11,... | collective-permute-start | bytes 49160 | tf_op jit(solution)/shard_map/ppermute | solution.py:27
  1.9 12.3 %collective-permute-start.1 = (bf16[2,32,128]{2,1,0:T(8,128)(2,1)S(1)}, bf16[2,32,128]{2,1,0:T(8,128)(2,1)S(1)}, u32[]{:S(2)}, u32[]{:S(2)}) collective-permute-start(bf16[2,32,128]{2,1,0:T(8,128)(2,1)S(1)} %get-tuple-element.19), channel_id=1, source_target_pairs={{0,1},{1,0},{2,3},{3,2},{4,5},{5,4},{6,7},{7,6},{8,9},{9,8},{10,11... | collective-permute-start | bytes 49160 | tf_op jit(solution)/shard_map/ppermute | solution.py:27
  15.6 11.0 %copy-start.3 = (f32[32,24,128]{2,1,0:T(8,128)S(1)}, f32[32,24,128]{2,1,0:T(8,128)}, u32[]{:S(2)}) copy-start(f32[32,24,128]{2,1,0:T(8,128)} %param.6) | copy-start | bytes 1179652
  15.6 11.0 %collective-permute-start.2 = (bf16[2,48,128]{2,1,0:T(8,128)(2,1)S(1)}, bf16[2,48,128]{2,1,0:T(8,128)(2,1)S(1)}, u32[]{:S(2)}, u32[]{:S(2)}) collective-permute-start(bf16[2,48,128]{2,1,0:T(8,128)(2,1)S(1)} %get-tuple-element.20), channel_id=1, source_target_pairs={{1,2},{2,1},{3,4},{4,3},{5,6},{6,5},{7,8},{8,7},{9,10},{10,9},{11,... | collective-permute-start | bytes 73736 | tf_op jit(solution)/shard_map/ppermute | solution.py:27
  16.4 10.2 %collective-permute-start.3 = (bf16[2,48,128]{2,1,0:T(8,128)(2,1)S(1)}, bf16[2,48,128]{2,1,0:T(8,128)(2,1)S(1)}, u32[]{:S(2)}, u32[]{:S(2)}) collective-permute-start(bf16[2,48,128]{2,1,0:T(8,128)(2,1)S(1)} %get-tuple-element.21), channel_id=1, source_target_pairs={{0,1},{1,0},{2,3},{3,2},{4,5},{5,4},{6,7},{7,6},{8,9},{9,8},{10,11... | collective-permute-start | bytes 73736 | tf_op jit(solution)/shard_map/ppermute | solution.py:27
  29.0 18.8 %all-to-all-start = ((bf16[16,2,24,128]{3,2,1,0:T(8,128)(2,1)}), bf16[16,2,24,128]{3,2,1,0:T(8,128)(2,1)S(1)}, u32[]{:S(2)}, u32[]{:S(2)}) async-start(bf16[16,2,24,128]{3,2,1,0:T(8,128)(2,1)} %get-tuple-element.30), calls=%async_computation | async-start | bytes 393216 | tf_op jit(solution)/shard_map/all_to_all | solution.py:221
  48.0 10.8 %collective-permute-start.4 = (bf16[2,24,128]{2,1,0:T(8,128)(2,1)S(1)}, bf16[2,24,128]{2,1,0:T(8,128)(2,1)S(1)}, u32[]{:S(2)}, u32[]{:S(2)}) collective-permute-start(bf16[2,24,128]{2,1,0:T(8,128)(2,1)S(1)} %get-tuple-element.32), channel_id=1, source_target_pairs={{0,256},{16,272},{32,288},{48,304},{64,320},{80,336},{96,352},{112... | collective-permute-start | bytes 36872 | tf_op jit(solution)/shard_map/ppermute | solution.py:236

commit v4 on v3

--- a/solution.py
+++ b/solution.py
@@ -69,16 +69,34 @@
     return jnp.concatenate([residual, tail], 0)
 
 
-def coupled_sum(j, at, picked, couple, blocks_ref):
-    rows = jnp.concatenate([picked[at + couple[s, j]] for s in range(SLOTS)], 1)
-    weights = jnp.concatenate([blocks_ref[s, j] for s in range(SLOTS)], 1)
-    return times_transposed(rows, weights)
+def pair_product(x, w):
+    rows = x[0].shape[0]
+    zero = jnp.zeros_like(x[0])
+    left = jnp.concatenate([jnp.concatenate([x[0], zero], 1), jnp.concatenate([zero, x[1]], 1)], 0)
+    both = times_transposed(left, jnp.concatenate(w, 1))
+    return both[:rows], both[rows:]
+
+
+def coupled_pair(j, at, picked, couple, blocks_ref):
+    deep = SLOTS - 1
+    last = pair_product(
+        [picked[at + k + couple[deep, j + k]] for k in range(2)],
+        [blocks_ref[deep, j + k] for k in range(2)],
+    )
+    total = []
+    for k in range(2):
+        rows = jnp.concatenate([picked[at + k + couple[s, j + k]] for s in range(deep)], 1)
+        weights = jnp.concatenate([blocks_ref[s, j + k] for s in range(deep)], 1)
+        total.append(times_transposed(rows, weights) + last[k])
+    return total
 
 
 def solve_source(j, flux, state_ref, forcing_ref, initial_ref, precond_ref):
-    rows = block_residual(j, flux, state_ref, forcing_ref, initial_ref)
-    smooth = times_transposed(rows.astype(jnp.bfloat16), precond_ref[j])
-    return 2.0 * rows - relaxation * smooth, smooth
+    rows = [block_residual(j + k, flux[k], state_ref, forcing_ref, initial_ref) for k in range(2)]
+    smooth = pair_product(
+        [r.astype(jnp.bfloat16) for r in rows], [precond_ref[j + k] for k in range(2)]
+    )
+    return [2.0 * rows[k] - relaxation * smooth[k] for k in range(2)], smooth
 
 
 def edge_squares(state_ref, send_first, send_second):
@@ -102,23 +120,25 @@
     width, steps, _ = squares.shape
     for j in range(width):
         squares[j] = squared(state_ref, j, width, steps)
-    for j in range(2, width - 2):
-        flux = coupled_sum(j, j, squares, couple, blocks_ref)
+    for j in range(2, width - 2, 2):
+        flux = coupled_pair(j, j, squares, couple, blocks_ref)
         outer, smooth = solve_source(j, flux, state_ref, forcing_ref, initial_ref, precond_ref)
-        outer_ref[j - 2] = outer
-        smooth_ref[j - 2] = smooth
+        for k in range(2):
+            outer_ref[j - 2 + k] = outer[k]
+            smooth_ref[j - 2 + k] = smooth[k]
 
 
 def source_edges(couple, first_ref, second_ref, state_ref, forcing_ref, initial_ref, blocks_ref, precond_ref, outer_ref, smooth_ref, send_first, send_second, windows):
     width = initial_ref.shape[0]
     steps = windows.shape[2]
     fill_windows(windows, first_ref, second_ref, lambda k: squared(state_ref, k, width, steps), width)
-    for e in range(4):
-        j = e if e < 2 else width - 4 + e
-        flux = coupled_sum(j, 2 + e % 2, windows.at[e // 2], couple, blocks_ref)
+    for e in range(2):
+        j = e * (width - 2)
+        flux = coupled_pair(j, 2, windows.at[e], couple, blocks_ref)
         outer, smooth = solve_source(j, flux, state_ref, forcing_ref, initial_ref, precond_ref)
-        outer_ref[e] = outer
-        smooth_ref[e] = smooth
+        for k in range(2):
+            outer_ref[2 * e + k] = outer[k]
+            smooth_ref[2 * e + k] = smooth[k]
 
     @pl.when(is_odd())
     def _():
@@ -131,22 +151,26 @@
         send_second[...] = smooth_ref[2:4].astype(jnp.bfloat16)
 
 
-def solve_block(j, coupled, outer, smooth, precond_ref, out_outer, out_inner, out_next, width):
-    rows = coupled.shape[0]
+def split(value):
+    high = value.astype(jnp.bfloat16)
+    return [high, (value - high.astype(jnp.float32)).astype(jnp.bfloat16)]
+
+
+def solve_pair(j, coupled, outer, smooth, precond_ref, out_outer, out_inner, out_next, width):
+    rows = coupled[0].shape[0]
     steps = rows - EXTRA
-    inner = relaxation * (smooth - time_step * coupled)
-    outer_high = outer.astype(jnp.bfloat16)
-    outer_low = (outer - outer_high.astype(jnp.float32)).astype(jnp.bfloat16)
-    inner_high = inner.astype(jnp.bfloat16)
-    inner_low = (inner - inner_high.astype(jnp.float32)).astype(jnp.bfloat16)
-    pieces = jnp.concatenate([outer_high, outer_low, inner_high, inner_low], 0)
-    solved = times_transposed(pieces, precond_ref[j])
-    outer = solved[:rows] + solved[rows : 2 * rows]
-    inner = solved[2 * rows : 3 * rows] + solved[3 * rows :]
-    out_outer[pl.ds(j, steps, stride=width), :] = outer[:steps]
-    out_inner[pl.ds(j, steps, stride=width), :] = inner[:steps]
-    out_next[pl.ds(j, 1), :] = outer[steps : steps + 1]
-    out_next[pl.ds(width + j, 1), :] = inner[steps : steps + 1]
+    pieces = []
+    for k in range(2):
+        inner = relaxation * (smooth[k] - time_step * coupled[k])
+        pieces.append(jnp.concatenate(split(outer[k]) + split(inner), 0))
+    solved = pair_product(pieces, [precond_ref[j + k] for k in range(2)])
+    for k in range(2):
+        outer_k = solved[k][:rows] + solved[k][rows : 2 * rows]
+        inner_k = solved[k][2 * rows : 3 * rows] + solved[k][3 * rows :]
+        out_outer[pl.ds(j + k, steps, stride=width), :] = outer_k[:steps]
+        out_inner[pl.ds(j + k, steps, stride=width), :] = inner_k[:steps]
+        out_next[pl.ds(j + k, 1), :] = outer_k[steps : steps + 1]
+        out_next[pl.ds(width + j + k, 1), :] = inner_k[steps : steps + 1]
 
 
 def solve_inside(couple, all_inside_ref, all_edges_ref, outer_ref, blocks_ref, precond_ref, out_outer, out_inner, out_next, rounded):
@@ -159,9 +183,11 @@
     out_outer[...] = jnp.zeros_like(out_outer)
     out_inner[...] = jnp.zeros_like(out_inner)
     out_next[...] = jnp.zeros_like(out_next)
-    for j in range(2, width - 2):
-        coupled = coupled_sum(j, j, rounded, couple, blocks_ref)
-        solve_block(j, coupled, outer_ref[j - 2], all_inside_ref[j - 2], precond_ref, out_outer, out_inner, out_next, width)
+    for j in range(2, width - 2, 2):
+        coupled = coupled_pair(j, j, rounded, couple, blocks_ref)
+        outer = [outer_ref[j - 2 + k] for k in range(2)]
+        smooth = [all_inside_ref[j - 2 + k] for k in range(2)]
+        solve_pair(j, coupled, outer, smooth, precond_ref, out_outer, out_inner, out_next, width)
 
 
 def solve_edges(couple, first_ref, second_ref, all_inside_ref, all_edges_ref, outer_ref, blocks_ref, precond_ref, in_outer, in_inner, in_next, state_ref, result_ref, ends_ref, windows, my_outer, my_inner, my_next):
@@ -179,10 +205,12 @@
     my_outer[...] = in_outer[...]
     my_inner[...] = in_inner[...]
     my_next[...] = in_next[...]
-    for e in range(4):
-        j = e if e < 2 else width - 4 + e
-        coupled = coupled_sum(j, 2 + e % 2, windows.at[e // 2], couple, blocks_ref)
-        solve_block(j, coupled, outer_ref[e], all_edges_ref[e], precond_ref, my_outer, my_inner, my_next, width)
+    for e in range(2):
+        j = e * (width - 2)
+        coupled = coupled_pair(j, 2, windows.at[e], couple, blocks_ref)
+        outer = [outer_ref[2 * e + k] for k in range(2)]
+        smooth = [all_edges_ref[2 * e + k] for k in range(2)]
+        solve_pair(j, coupled, outer, smooth, precond_ref, my_outer, my_inner, my_next, width)
     z = jnp.zeros((width, 128), jnp.float32)
     y = jnp.zeros((width, 128), jnp.float32)
     for n in range(steps):

time: 60.1 us -> 58 us (0.965)
  Pallas kernels: 13.5 us -> 11.3 us
    pallas_call x6, Pallas kernels: 13.5 us -> 11.3 us  [run(): pl.pallas_call(kernel, out_shape=results, in_specs=scalar + [vector] * (l...]
  transfers between devices with their start and end apart: 6 -> 6, of which waited for: 2 -> 2; matrix products, arithmetic and copies ran while one was open for 0% -> 0% of each run, Pallas kernels for 15% -> 12%
where the time goes in v4:
time: 58 us; the launch traced here: 57.6 us
  starting transfers between devices  33.1 us (57%)
  Pallas kernels  11.3 us (19%)
  waiting for transfers between devices  10.8 us (19%)
  between operations  1.06 us (2%)
  local copies, waits for them, and re-layouts  1.02 us (2%)
    ppermute x2, starting transfers between devices, exchange(): lax.ppermute(second_edge, axis, second)  13.5 us
    pallas_call x6, Pallas kernels, run(): pl.pallas_call(kernel, out_shape=results, in_specs=scalar + [vector] * (l...  11.3 us
    all_to_all x1, waiting for transfers between devices, ring_carry(): lax.all_to_all(sent, 'tm', 0, 0, axis_index_groups=members, tiled=True)  9.42 us
    ppermute x1, starting transfers between devices, ring_carry(): other = lax.ppermute(total, 'tm', route)  9.39 us
    all_to_all x1, starting transfers between devices, ring_carry(): lax.all_to_all(sent, 'tm', 0, 0, axis_index_groups=members, tiled=True)  8.63 us
    ppermute x2, starting transfers between devices, exchange(): lax.ppermute(first_edge, axis, first)  1.59 us
    ppermute x1, waiting for transfers between devices, ring_carry(): other = lax.ppermute(total, 'tm', route)  1.31 us
  transfers between devices with their start and end apart: 6, of which 2 were waited for; matrix products, arithmetic and copies ran while one was open for 0% of the time, Pallas kernels for 12%

profile of v4, /device:TPU:1, one launch (start us, length us, event | category | flops | bytes accessed | tf_op | source)
XLA Modules:
  0.0 57.6 jit_solution(5673806459349362351)
XLA Ops:
  0.0 0.0 copy-start.2
  0.0 1.0 %copy-done.2 = f32[32,24,128]{2,1,0:T(8,128)S(1)} copy-done((f32[32,24,128]{2,1,0:T(8,128)S(1)}, f32[32,24,128]{2,1,0:T(8,128)}, u32[]{:S(2)}) %copy-start.2) | copy-done | bytes 393240
  1.0 0.0 copy-start
  1.0 0.0 copy-start.1
  1.0 0.0 copy-start.4
  1.0 0.0 copy-start.5
  1.0 0.0 copy-start.6
  1.1 0.8 %collective-permute-start = (bf16[2,32,128]{2,1,0:T(8,128)(2,1)S(1)}, bf16[2,32,128]{2,1,0:T(8,128)(2,1)S(1)}, u32[]{:S(2)}, u32[]{:S(2)}) collective-permute-start(bf16[2,32,128]{2,1,0:T(8,128)(2,1)S(1)} %get-tuple-element.18), channel_id=1, source_target_pairs={{1,2},{2,1},{3,4},{4,3},{5,6},{6,5},{7,8},{8,7},{9,10},{10,9},{11,... | collective-permute-start | bytes 49160 | tf_op jit(solution)/shard_map/ppermute | solution.py:27
  1.9 8.3 %collective-permute-start.1 = (bf16[2,32,128]{2,1,0:T(8,128)(2,1)S(1)}, bf16[2,32,128]{2,1,0:T(8,128)(2,1)S(1)}, u32[]{:S(2)}, u32[]{:S(2)}) collective-permute-start(bf16[2,32,128]{2,1,0:T(8,128)(2,1)S(1)} %get-tuple-element.19), channel_id=1, source_target_pairs={{0,1},{1,0},{2,3},{3,2},{4,5},{5,4},{6,7},{7,6},{8,9},{9,8},{10,11... | collective-permute-start | bytes 49160 | tf_op jit(solution)/shard_map/ppermute | solution.py:27
  10.2 0.0 copy-done
  10.2 0.0 copy-done.1
  10.2 0.0 copy-done.4
  10.2 0.0 copy-done.5
  10.2 0.0 copy-done.6
  10.2 3.5 %source_inside.1 = (f32[20,48,128]{2,1,0:T(8,128)S(1)}, f32[20,48,128]{2,1,0:T(8,128)S(1)}) custom-call(s32[5,24]{1,0:T(8,128)S(1)} %bitcast.166, f32[768,128]{1,0:T(8,128)S(1)} %bitcast.161, f32[768,128]{1,0:T(8,128)S(1)} %bitcast.164, f32[24,128]{1,0:T(8,128)S(1)} %copy-done.6, bf16[5,24,128,128]{3,2,1,0:T(8,128)(2,1)S(1)} %copy-done, ...), custom_call_target="tpu_custom_call" | custom-call | flops 188743680 | bytes 4932160 | tf_op jit(solution)/shard_map/source_inside/pallas_call | solution.py:287
  13.7 0.0 collective-permute-done.first_ref
  13.7 0.0 collective-permute-done.1.second_ref
  13.7 1.3 %source_edges.1 = (f32[4,48,128]{2,1,0:T(8,128)S(1)}, f32[4,48,128]{2,1,0:T(8,128)S(1)}, bf16[2,48,128]{2,1,0:T(8,128)(2,1)S(1)}, bf16[2,48,128]{2,1,0:T(8,128)(2,1)S(1)}) custom-call(s32[5,24]{1,0:T(8,128)S(1)} %bitcast.167, bf16[2,32,128]{2,1,0:T(8,128)(2,1)S(1)} %collective-permute-done.first_ref, ...), custom_call_target="tpu_custom_call" | custom-call | flops 37748736 | bytes 1786432 | tf_op jit(solution)/shard_map/source_edges/pallas_call | solution.py:287
  15.1 0.0 copy-start.3
  15.1 0.8 %collective-permute-start.2 = (bf16[2,48,128]{2,1,0:T(8,128)(2,1)S(1)}, bf16[2,48,128]{2,1,0:T(8,128)(2,1)S(1)}, u32[]{:S(2)}, u32[]{:S(2)}) collective-permute-start(bf16[2,48,128]{2,1,0:T(8,128)(2,1)S(1)} %get-tuple-element.20), channel_id=1, source_target_pairs={{1,2},{2,1},{3,4},{4,3},{5,6},{6,5},{7,8},{8,7},{9,10},{10,9},{11,... | collective-permute-start | bytes 73736 | tf_op jit(solution)/shard_map/ppermute | solution.py:27
  15.9 5.3 %collective-permute-start.3 = (bf16[2,48,128]{2,1,0:T(8,128)(2,1)S(1)}, bf16[2,48,128]{2,1,0:T(8,128)(2,1)S(1)}, u32[]{:S(2)}, u32[]{:S(2)}) collective-permute-start(bf16[2,48,128]{2,1,0:T(8,128)(2,1)S(1)} %get-tuple-element.21), channel_id=1, source_target_pairs={{0,1},{1,0},{2,3},{3,2},{4,5},{5,4},{6,7},{7,6},{8,9},{9,8},{10,11... | collective-permute-start | bytes 73736 | tf_op jit(solution)/shard_map/ppermute | solution.py:27
  21.1 3.6 %solve_inside.1 = (f32[768,128]{1,0:T(8,128)S(1)}, f32[768,128]{1,0:T(8,128)S(1)}, f32[48,128]{1,0:T(8,128)S(1)}) custom-call(s32[5,24]{1,0:T(8,128)S(1)} %bitcast.168, f32[20,48,128]{2,1,0:T(8,128)S(1)} %get-tuple-element.22.all_inside_ref, f32[4,48,128]{2,1,0:T(8,128)S(1)} %get-tuple-element.23.all_edges_ref, ...), custom_call_target="tpu_custom_call" | custom-call | flops 283115520 | bytes 4932160 | tf_op jit(solution)/shard_map/solve_inside/pallas_call | solution.py:287
  24.7 0.0 collective-permute-done.2.first_ref
  24.7 0.0 collective-permute-done.3.second_ref
  24.8 0.0 copy-done.3
  24.8 2.1 %solve_edges.1 = (f32[768,128]{1,0:T(8,128)S(1)}, bf16[16,2,24,128]{3,2,1,0:T(8,128)(2,1)}) custom-call(s32[5,24]{1,0:T(8,128)S(1)} %bitcast.169, bf16[2,48,128]{2,1,0:T(8,128)(2,1)S(1)} %collective-permute-done.2.first_ref, bf16[2,48,128]{2,1,0:T(8,128)(2,1)S(1)} %collective-permute-done.3.second_ref, f32[20,48,128]{2,1,0:T(8,128)S(1)} %get-tuple-element.22.all_inside_ref, ...), custom_call_target="tpu_custom_call" | custom-call | flops 56623104 | bytes 1786432 | tf_op jit(solution)/shard_map/solve_edges/pallas_call | solution.py:287
  26.9 8.6 %all-to-all-start = ((bf16[16,2,24,128]{3,2,1,0:T(8,128)(2,1)}), bf16[16,2,24,128]{3,2,1,0:T(8,128)(2,1)S(1)}, u32[]{:S(2)}, u32[]{:S(2)}) async-start(bf16[16,2,24,128]{3,2,1,0:T(8,128)(2,1)} %get-tuple-element.30), calls=%async_computation | async-start | bytes 393216 | tf_op jit(solution)/shard_map/all_to_all | solution.py:249
  36.3 9.4 %all-to-all-done = bf16[16,2,24,128]{3,2,1,0:T(8,128)(2,1)S(1)} async-done(((bf16[16,2,24,128]{3,2,1,0:T(8,128)(2,1)}), bf16[16,2,24,128]{3,2,1,0:T(8,128)(2,1)S(1)}, u32[]{:S(2)}, u32[]{:S(2)}) %all-to-all-start) | async-done | bytes 196640 | tf_op jit(solution)/shard_map/all_to_all | solution.py:249
  45.9 9.4 %collective-permute-start.4 = (bf16[2,24,128]{2,1,0:T(8,128)(2,1)S(1)}, bf16[2,24,128]{2,1,0:T(8,128)(2,1)S(1)}, u32[]{:S(2)}, u32[]{:S(2)}) collective-permute-start(bf16[2,24,128]{2,1,0:T(8,128)(2,1)S(1)} %get-tuple-element.32), channel_id=1, source_target_pairs={{0,256},{16,272},{32,288},{48,304},{64,320},{80,336},{96,352},{112... | collective-permute-start | bytes 36872 | tf_op jit(solution)/shard_map/ppermute | solution.py:264
  55.4 1.3 %collective-permute-done.4 = bf16[2,24,128]{2,1,0:T(8,128)(2,1)S(1)} collective-permute-done((bf16[2,24,128]{2,1,0:T(8,128)(2,1)S(1)}, bf16[2,24,128]{2,1,0:T(8,128)(2,1)S(1)}, u32[]{:S(2)}, u32[]{:S(2)}) %collective-permute-start.4) | collective-permute-done | bytes 12320 | tf_op jit(solution)/shard_map/ppermute | solution.py:264
  56.7 0.1 fusion.15.carry_ref
  56.8 0.8 %finish_kernel.1 = f32[768,128]{1,0:T(8,128)} custom-call(f32[768,128]{1,0:T(8,128)S(1)} %get-tuple-element.29.local_ref, f32[2,24,128]{2,1,0:T(8,128)S(1)} %fusion.15.carry_ref), custom_call_target="tpu_custom_call" | custom-call | flops 1572864 | bytes 1196608 | tf_op jit(solution)/shard_map/finish_kernel/pallas_call | solution.py:287
  (17 shorter events, 0.3 us)
Async XLA Ops:
  0.0 1.0 %copy-start.2 = (f32[32,24,128]{2,1,0:T(8,128)S(1)}, f32[32,24,128]{2,1,0:T(8,128)}, u32[]{:S(2)}) copy-start(f32[32,24,128]{2,1,0:T(8,128)} %param.6) | copy-start | bytes 1179652
  1.0 9.2 %copy-start = (bf16[5,24,128,128]{3,2,1,0:T(8,128)(2,1)S(1)}, bf16[5,24,128,128]{3,2,1,0:T(8,128)(2,1)}, u32[]{:S(2)}) copy-start(bf16[5,24,128,128]{3,2,1,0:T(8,128)(2,1)} %blocks_ref.7) | copy-start | bytes 11796484
  1.0 9.2 %copy-start.1 = (bf16[24,128,128]{2,1,0:T(8,128)(2,1)S(1)}, bf16[24,128,128]{2,1,0:T(8,128)(2,1)}, u32[]{:S(2)}) copy-start(bf16[24,128,128]{2,1,0:T(8,128)(2,1)} %precond_ref.7) | copy-start | bytes 2359300
  1.0 9.2 %copy-start.4 = (f32[32,24,128]{2,1,0:T(8,128)S(1)}, f32[32,24,128]{2,1,0:T(8,128)}, u32[]{:S(2)}) copy-start(f32[32,24,128]{2,1,0:T(8,128)} %param.7) | copy-start | bytes 1179652
  1.0 9.2 %copy-start.5 = (s32[24,5]{0,1:T(8,128)S(1)}, s32[24,5]{0,1:T(8,128)}, u32[]{:S(2)}) copy-start(s32[24,5]{0,1:T(8,128)} %param.11) | copy-start | bytes 1444
  1.0 9.2 %copy-start.6 = (f32[24,128]{1,0:T(8,128)S(1)}, f32[24,128]{1,0:T(8,128)}, u32[]{:S(2)}) copy-start(f32[24,128]{1,0:T(8,128)} %initial_ref.3) | copy-start | bytes 36868
  1.1 12.7 %collective-permute-start = (bf16[2,32,128]{2,1,0:T(8,128)(2,1)S(1)}, bf16[2,32,128]{2,1,0:T(8,128)(2,1)S(1)}, u32[]{:S(2)}, u32[]{:S(2)}) collective-permute-start(bf16[2,32,128]{2,1,0:T(8,128)(2,1)S(1)} %get-tuple-element.18), channel_id=1, source_target_pairs={{1,2},{2,1},{3,4},{4,3},{5,6},{6,5},{7,8},{8,7},{9,10},{10,9},{11,... | collective-permute-start | bytes 49160 | tf_op jit(solution)/shard_map/ppermute | solution.py:27
  1.9 11.9 %collective-permute-start.1 = (bf16[2,32,128]{2,1,0:T(8,128)(2,1)S(1)}, bf16[2,32,128]{2,1,0:T(8,128)(2,1)S(1)}, u32[]{:S(2)}, u32[]{:S(2)}) collective-permute-start(bf16[2,32,128]{2,1,0:T(8,128)(2,1)S(1)} %get-tuple-element.19), channel_id=1, source_target_pairs={{0,1},{1,0},{2,3},{3,2},{4,5},{5,4},{6,7},{7,6},{8,9},{9,8},{10,11... | collective-permute-start | bytes 49160 | tf_op jit(solution)/shard_map/ppermute | solution.py:27
  15.1 9.7 %copy-start.3 = (f32[32,24,128]{2,1,0:T(8,128)S(1)}, f32[32,24,128]{2,1,0:T(8,128)}, u32[]{:S(2)}) copy-start(f32[32,24,128]{2,1,0:T(8,128)} %param.6) | copy-start | bytes 1179652
  15.1 9.7 %collective-permute-start.2 = (bf16[2,48,128]{2,1,0:T(8,128)(2,1)S(1)}, bf16[2,48,128]{2,1,0:T(8,128)(2,1)S(1)}, u32[]{:S(2)}, u32[]{:S(2)}) collective-permute-start(bf16[2,48,128]{2,1,0:T(8,128)(2,1)S(1)} %get-tuple-element.20), channel_id=1, source_target_pairs={{1,2},{2,1},{3,4},{4,3},{5,6},{6,5},{7,8},{8,7},{9,10},{10,9},{11,... | collective-permute-start | bytes 73736 | tf_op jit(solution)/shard_map/ppermute | solution.py:27
  15.9 8.9 %collective-permute-start.3 = (bf16[2,48,128]{2,1,0:T(8,128)(2,1)S(1)}, bf16[2,48,128]{2,1,0:T(8,128)(2,1)S(1)}, u32[]{:S(2)}, u32[]{:S(2)}) collective-permute-start(bf16[2,48,128]{2,1,0:T(8,128)(2,1)S(1)} %get-tuple-element.21), channel_id=1, source_target_pairs={{0,1},{1,0},{2,3},{3,2},{4,5},{5,4},{6,7},{7,6},{8,9},{9,8},{10,11... | collective-permute-start | bytes 73736 | tf_op jit(solution)/shard_map/ppermute | solution.py:27
  26.9 18.8 %all-to-all-start = ((bf16[16,2,24,128]{3,2,1,0:T(8,128)(2,1)}), bf16[16,2,24,128]{3,2,1,0:T(8,128)(2,1)S(1)}, u32[]{:S(2)}, u32[]{:S(2)}) async-start(bf16[16,2,24,128]{3,2,1,0:T(8,128)(2,1)} %get-tuple-element.30), calls=%async_computation | async-start | bytes 393216 | tf_op jit(solution)/shard_map/all_to_all | solution.py:249
  45.9 10.8 %collective-permute-start.4 = (bf16[2,24,128]{2,1,0:T(8,128)(2,1)S(1)}, bf16[2,24,128]{2,1,0:T(8,128)(2,1)S(1)}, u32[]{:S(2)}, u32[]{:S(2)}) collective-permute-start(bf16[2,24,128]{2,1,0:T(8,128)(2,1)S(1)} %get-tuple-element.32), channel_id=1, source_target_pairs={{0,256},{16,272},{32,288},{48,304},{64,320},{80,336},{96,352},{112... | collective-permute-start | bytes 36872 | tf_op jit(solution)/shard_map/ppermute | solution.py:264

commit v5 on v4

--- a/solution.py
+++ b/solution.py
@@ -120,8 +120,11 @@
     width, steps, _ = squares.shape
     for j in range(width):
         squares[j] = squared(state_ref, j, width, steps)
+    ahead = coupled_pair(2, 2, squares, couple, blocks_ref)
     for j in range(2, width - 2, 2):
-        flux = coupled_pair(j, j, squares, couple, blocks_ref)
+        flux = ahead
+        if j + 2 < width - 2:
+            ahead = coupled_pair(j + 2, j + 2, squares, couple, blocks_ref)
         outer, smooth = solve_source(j, flux, state_ref, forcing_ref, initial_ref, precond_ref)
         for k in range(2):
             outer_ref[j - 2 + k] = outer[k]
@@ -132,10 +135,12 @@
     width = initial_ref.shape[0]
     steps = windows.shape[2]
     fill_windows(windows, first_ref, second_ref, lambda k: squared(state_ref, k, width, steps), width)
+    fluxes = [
+        coupled_pair(e * (width - 2), 2, windows.at[e], couple, blocks_ref) for e in range(2)
+    ]
     for e in range(2):
         j = e * (width - 2)
-        flux = coupled_pair(j, 2, windows.at[e], couple, blocks_ref)
-        outer, smooth = solve_source(j, flux, state_ref, forcing_ref, initial_ref, precond_ref)
+        outer, smooth = solve_source(j, fluxes[e], state_ref, forcing_ref, initial_ref, precond_ref)
         for k in range(2):
             outer_ref[2 * e + k] = outer[k]
             smooth_ref[2 * e + k] = smooth[k]
@@ -183,8 +188,11 @@
     out_outer[...] = jnp.zeros_like(out_outer)
     out_inner[...] = jnp.zeros_like(out_inner)
     out_next[...] = jnp.zeros_like(out_next)
+    ahead = coupled_pair(2, 2, rounded, couple, blocks_ref)
     for j in range(2, width - 2, 2):
-        coupled = coupled_pair(j, j, rounded, couple, blocks_ref)
+        coupled = ahead
+        if j + 2 < width - 2:
+            ahead = coupled_pair(j + 2, j + 2, rounded, couple, blocks_ref)
         outer = [outer_ref[j - 2 + k] for k in range(2)]
         smooth = [all_inside_ref[j - 2 + k] for k in range(2)]
         solve_pair(j, coupled, outer, smooth, precond_ref, out_outer, out_inner, out_next, width)
@@ -205,12 +213,14 @@
     my_outer[...] = in_outer[...]
     my_inner[...] = in_inner[...]
     my_next[...] = in_next[...]
+    coupled = [
+        coupled_pair(e * (width - 2), 2, windows.at[e], couple, blocks_ref) for e in range(2)
+    ]
     for e in range(2):
         j = e * (width - 2)
-        coupled = coupled_pair(j, 2, windows.at[e], couple, blocks_ref)
         outer = [outer_ref[2 * e + k] for k in range(2)]
         smooth = [all_edges_ref[2 * e + k] for k in range(2)]
-        solve_pair(j, coupled, outer, smooth, precond_ref, my_outer, my_inner, my_next, width)
+        solve_pair(j, coupled[e], outer, smooth, precond_ref, my_outer, my_inner, my_next, width)
     z = jnp.zeros((width, 128), jnp.float32)
     y = jnp.zeros((width, 128), jnp.float32)
     for n in range(steps):

time: 58 us -> 55.9 us (0.964); the launches traced: 57.6 us -> 54.8 us
  Pallas kernels: 11.3 us -> 8.5 us
    pallas_call x6, Pallas kernels: 11.3 us -> 8.5 us  [run(): pl.pallas_call(kernel, out_shape=results, in_specs=scalar + [vector] * (l...]
  transfers between devices with their start and end apart: 6 -> 6, of which waited for: 2 -> 2; matrix products, arithmetic and copies ran while one was open for 0% -> 0% of each run, Pallas kernels for 12% -> 9%
where the time goes in v5:
time: 55.9 us; the launch traced here: 54.8 us
  starting transfers between devices  33.2 us (59%)
  waiting for transfers between devices  10.8 us (19%)
  Pallas kernels  8.5 us (15%)
  between operations  1.06 us (2%)
  local copies, waits for them, and re-layouts  1.02 us (2%)
    ppermute x2, starting transfers between devices, exchange(): lax.ppermute(second_edge, axis, second)  13.6 us
    all_to_all x1, waiting for transfers between devices, ring_carry(): lax.all_to_all(sent, 'tm', 0, 0, axis_index_groups=members, tiled=True)  9.42 us
    ppermute x1, starting transfers between devices, ring_carry(): other = lax.ppermute(total, 'tm', route)  9.4 us
    all_to_all x1, starting transfers between devices, ring_carry(): lax.all_to_all(sent, 'tm', 0, 0, axis_index_groups=members, tiled=True)  8.62 us
    pallas_call x6, Pallas kernels, run(): pl.pallas_call(kernel, out_shape=results, in_specs=scalar + [vector] * (l...  8.5 us
    ppermute x2, starting transfers between devices, exchange(): lax.ppermute(first_edge, axis, first)  1.59 us
    ppermute x1, waiting for transfers between devices, ring_carry(): other = lax.ppermute(total, 'tm', route)  1.31 us
  transfers between devices with their start and end apart: 6, of which 2 were waited for; matrix products, arithmetic and copies ran while one was open for 0% of the time, Pallas kernels for 9%

profile of v5, /device:TPU:1, one launch (start us, length us, event | category | flops | bytes accessed | tf_op | source)
XLA Modules:
  0.0 54.8 jit_solution(13724200927755836565)
XLA Ops:
  0.0 0.0 copy-start.2
  0.0 1.0 %copy-done.2 = f32[32,24,128]{2,1,0:T(8,128)S(1)} copy-done((f32[32,24,128]{2,1,0:T(8,128)S(1)}, f32[32,24,128]{2,1,0:T(8,128)}, u32[]{:S(2)}) %copy-start.2) | copy-done | bytes 393240
  1.0 0.0 copy-start
  1.0 0.0 copy-start.1
  1.0 0.0 copy-start.4
  1.0 0.0 copy-start.5
  1.0 0.0 copy-start.6
  1.1 0.8 %collective-permute-start = (bf16[2,32,128]{2,1,0:T(8,128)(2,1)S(1)}, bf16[2,32,128]{2,1,0:T(8,128)(2,1)S(1)}, u32[]{:S(2)}, u32[]{:S(2)}) collective-permute-start(bf16[2,32,128]{2,1,0:T(8,128)(2,1)S(1)} %get-tuple-element.18), channel_id=1, source_target_pairs={{1,2},{2,1},{3,4},{4,3},{5,6},{6,5},{7,8},{8,7},{9,10},{10,9},{11,... | collective-permute-start | bytes 49160 | tf_op jit(solution)/shard_map/ppermute | solution.py:27
  1.9 8.3 %collective-permute-start.1 = (bf16[2,32,128]{2,1,0:T(8,128)(2,1)S(1)}, bf16[2,32,128]{2,1,0:T(8,128)(2,1)S(1)}, u32[]{:S(2)}, u32[]{:S(2)}) collective-permute-start(bf16[2,32,128]{2,1,0:T(8,128)(2,1)S(1)} %get-tuple-element.19), channel_id=1, source_target_pairs={{0,1},{1,0},{2,3},{3,2},{4,5},{5,4},{6,7},{7,6},{8,9},{9,8},{10,11... | collective-permute-start | bytes 49160 | tf_op jit(solution)/shard_map/ppermute | solution.py:27
  10.2 0.0 copy-done
  10.2 0.0 copy-done.1
  10.2 0.0 copy-done.4
  10.2 0.0 copy-done.5
  10.2 0.0 copy-done.6
  10.2 2.3 %source_inside.1 = (f32[20,48,128]{2,1,0:T(8,128)S(1)}, f32[20,48,128]{2,1,0:T(8,128)S(1)}) custom-call(s32[5,24]{1,0:T(8,128)S(1)} %bitcast.166, f32[768,128]{1,0:T(8,128)S(1)} %bitcast.161, f32[768,128]{1,0:T(8,128)S(1)} %bitcast.164, f32[24,128]{1,0:T(8,128)S(1)} %copy-done.6, bf16[5,24,128,128]{3,2,1,0:T(8,128)(2,1)S(1)} %copy-done, ...), custom_call_target="tpu_custom_call" | custom-call | flops 188743680 | bytes 4932160 | tf_op jit(solution)/shard_map/source_inside/pallas_call | solution.py:297
  12.5 0.0 collective-permute-done.first_ref
  12.5 0.0 collective-permute-done.1.second_ref
  12.5 1.1 %source_edges.1 = (f32[4,48,128]{2,1,0:T(8,128)S(1)}, f32[4,48,128]{2,1,0:T(8,128)S(1)}, bf16[2,48,128]{2,1,0:T(8,128)(2,1)S(1)}, bf16[2,48,128]{2,1,0:T(8,128)(2,1)S(1)}) custom-call(s32[5,24]{1,0:T(8,128)S(1)} %bitcast.167, bf16[2,32,128]{2,1,0:T(8,128)(2,1)S(1)} %collective-permute-done.first_ref, ...), custom_call_target="tpu_custom_call" | custom-call | flops 37748736 | bytes 1786432 | tf_op jit(solution)/shard_map/source_edges/pallas_call | solution.py:297
  13.6 0.0 copy-start.3
  13.6 0.8 %collective-permute-start.2 = (bf16[2,48,128]{2,1,0:T(8,128)(2,1)S(1)}, bf16[2,48,128]{2,1,0:T(8,128)(2,1)S(1)}, u32[]{:S(2)}, u32[]{:S(2)}) collective-permute-start(bf16[2,48,128]{2,1,0:T(8,128)(2,1)S(1)} %get-tuple-element.20), channel_id=1, source_target_pairs={{1,2},{2,1},{3,4},{4,3},{5,6},{6,5},{7,8},{8,7},{9,10},{10,9},{11,... | collective-permute-start | bytes 73736 | tf_op jit(solution)/shard_map/ppermute | solution.py:27
  14.4 5.3 %collective-permute-start.3 = (bf16[2,48,128]{2,1,0:T(8,128)(2,1)S(1)}, bf16[2,48,128]{2,1,0:T(8,128)(2,1)S(1)}, u32[]{:S(2)}, u32[]{:S(2)}) collective-permute-start(bf16[2,48,128]{2,1,0:T(8,128)(2,1)S(1)} %get-tuple-element.21), channel_id=1, source_target_pairs={{0,1},{1,0},{2,3},{3,2},{4,5},{5,4},{6,7},{7,6},{8,9},{9,8},{10,11... | collective-permute-start | bytes 73736 | tf_op jit(solution)/shard_map/ppermute | solution.py:27
  19.7 2.4 %solve_inside.1 = (f32[768,128]{1,0:T(8,128)S(1)}, f32[768,128]{1,0:T(8,128)S(1)}, f32[48,128]{1,0:T(8,128)S(1)}) custom-call(s32[5,24]{1,0:T(8,128)S(1)} %bitcast.168, f32[20,48,128]{2,1,0:T(8,128)S(1)} %get-tuple-element.22.all_inside_ref, f32[4,48,128]{2,1,0:T(8,128)S(1)} %get-tuple-element.23.all_edges_ref, ...), custom_call_target="tpu_custom_call" | custom-call | flops 283115520 | bytes 4932160 | tf_op jit(solution)/shard_map/solve_inside/pallas_call | solution.py:297
  22.1 0.0 collective-permute-done.2.first_ref
  22.1 0.0 collective-permute-done.3.second_ref
  22.1 0.0 copy-done.3
  22.2 1.9 %solve_edges.1 = (f32[768,128]{1,0:T(8,128)S(1)}, bf16[16,2,24,128]{3,2,1,0:T(8,128)(2,1)}) custom-call(s32[5,24]{1,0:T(8,128)S(1)} %bitcast.169, bf16[2,48,128]{2,1,0:T(8,128)(2,1)S(1)} %collective-permute-done.2.first_ref, bf16[2,48,128]{2,1,0:T(8,128)(2,1)S(1)} %collective-permute-done.3.second_ref, f32[20,48,128]{2,1,0:T(8,128)S(1)} %get-tuple-element.22.all_inside_ref, ...), custom_call_target="tpu_custom_call" | custom-call | flops 56623104 | bytes 1786432 | tf_op jit(solution)/shard_map/solve_edges/pallas_call | solution.py:297
  24.0 8.6 %all-to-all-start = ((bf16[16,2,24,128]{3,2,1,0:T(8,128)(2,1)}), bf16[16,2,24,128]{3,2,1,0:T(8,128)(2,1)S(1)}, u32[]{:S(2)}, u32[]{:S(2)}) async-start(bf16[16,2,24,128]{3,2,1,0:T(8,128)(2,1)} %get-tuple-element.30), calls=%async_computation | async-start | bytes 393216 | tf_op jit(solution)/shard_map/all_to_all | solution.py:259
  33.4 9.4 %all-to-all-done = bf16[16,2,24,128]{3,2,1,0:T(8,128)(2,1)S(1)} async-done(((bf16[16,2,24,128]{3,2,1,0:T(8,128)(2,1)}), bf16[16,2,24,128]{3,2,1,0:T(8,128)(2,1)S(1)}, u32[]{:S(2)}, u32[]{:S(2)}) %all-to-all-start) | async-done | bytes 196640 | tf_op jit(solution)/shard_map/all_to_all | solution.py:259
  43.0 9.4 %collective-permute-start.4 = (bf16[2,24,128]{2,1,0:T(8,128)(2,1)S(1)}, bf16[2,24,128]{2,1,0:T(8,128)(2,1)S(1)}, u32[]{:S(2)}, u32[]{:S(2)}) collective-permute-start(bf16[2,24,128]{2,1,0:T(8,128)(2,1)S(1)} %get-tuple-element.32), channel_id=1, source_target_pairs={{0,256},{16,272},{32,288},{48,304},{64,320},{80,336},{96,352},{112... | collective-permute-start | bytes 36872 | tf_op jit(solution)/shard_map/ppermute | solution.py:274
  52.5 1.3 %collective-permute-done.4 = bf16[2,24,128]{2,1,0:T(8,128)(2,1)S(1)} collective-permute-done((bf16[2,24,128]{2,1,0:T(8,128)(2,1)S(1)}, bf16[2,24,128]{2,1,0:T(8,128)(2,1)S(1)}, u32[]{:S(2)}, u32[]{:S(2)}) %collective-permute-start.4) | collective-permute-done | bytes 12320 | tf_op jit(solution)/shard_map/ppermute | solution.py:274
  53.9 0.1 fusion.15.carry_ref
  54.0 0.8 %finish_kernel.1 = f32[768,128]{1,0:T(8,128)} custom-call(f32[768,128]{1,0:T(8,128)S(1)} %get-tuple-element.29.local_ref, f32[2,24,128]{2,1,0:T(8,128)S(1)} %fusion.15.carry_ref), custom_call_target="tpu_custom_call" | custom-call | flops 1572864 | bytes 1196608 | tf_op jit(solution)/shard_map/finish_kernel/pallas_call | solution.py:297
  (17 shorter events, 0.3 us)
Async XLA Ops:
  0.0 1.0 %copy-start.2 = (f32[32,24,128]{2,1,0:T(8,128)S(1)}, f32[32,24,128]{2,1,0:T(8,128)}, u32[]{:S(2)}) copy-start(f32[32,24,128]{2,1,0:T(8,128)} %param.6) | copy-start | bytes 1179652
  1.0 9.2 %copy-start = (bf16[5,24,128,128]{3,2,1,0:T(8,128)(2,1)S(1)}, bf16[5,24,128,128]{3,2,1,0:T(8,128)(2,1)}, u32[]{:S(2)}) copy-start(bf16[5,24,128,128]{3,2,1,0:T(8,128)(2,1)} %blocks_ref.7) | copy-start | bytes 11796484
  1.0 9.2 %copy-start.1 = (bf16[24,128,128]{2,1,0:T(8,128)(2,1)S(1)}, bf16[24,128,128]{2,1,0:T(8,128)(2,1)}, u32[]{:S(2)}) copy-start(bf16[24,128,128]{2,1,0:T(8,128)(2,1)} %precond_ref.7) | copy-start | bytes 2359300
  1.0 9.2 %copy-start.4 = (f32[32,24,128]{2,1,0:T(8,128)S(1)}, f32[32,24,128]{2,1,0:T(8,128)}, u32[]{:S(2)}) copy-start(f32[32,24,128]{2,1,0:T(8,128)} %param.7) | copy-start | bytes 1179652
  1.0 9.2 %copy-start.5 = (s32[24,5]{0,1:T(8,128)S(1)}, s32[24,5]{0,1:T(8,128)}, u32[]{:S(2)}) copy-start(s32[24,5]{0,1:T(8,128)} %param.11) | copy-start | bytes 1444
  1.0 9.2 %copy-start.6 = (f32[24,128]{1,0:T(8,128)S(1)}, f32[24,128]{1,0:T(8,128)}, u32[]{:S(2)}) copy-start(f32[24,128]{1,0:T(8,128)} %initial_ref.3) | copy-start | bytes 36868
  1.1 11.4 %collective-permute-start = (bf16[2,32,128]{2,1,0:T(8,128)(2,1)S(1)}, bf16[2,32,128]{2,1,0:T(8,128)(2,1)S(1)}, u32[]{:S(2)}, u32[]{:S(2)}) collective-permute-start(bf16[2,32,128]{2,1,0:T(8,128)(2,1)S(1)} %get-tuple-element.18), channel_id=1, source_target_pairs={{1,2},{2,1},{3,4},{4,3},{5,6},{6,5},{7,8},{8,7},{9,10},{10,9},{11,... | collective-permute-start | bytes 49160 | tf_op jit(solution)/shard_map/ppermute | solution.py:27
  1.9 10.6 %collective-permute-start.1 = (bf16[2,32,128]{2,1,0:T(8,128)(2,1)S(1)}, bf16[2,32,128]{2,1,0:T(8,128)(2,1)S(1)}, u32[]{:S(2)}, u32[]{:S(2)}) collective-permute-start(bf16[2,32,128]{2,1,0:T(8,128)(2,1)S(1)} %get-tuple-element.19), channel_id=1, source_target_pairs={{0,1},{1,0},{2,3},{3,2},{4,5},{5,4},{6,7},{7,6},{8,9},{9,8},{10,11... | collective-permute-start | bytes 49160 | tf_op jit(solution)/shard_map/ppermute | solution.py:27
  13.6 8.6 %copy-start.3 = (f32[32,24,128]{2,1,0:T(8,128)S(1)}, f32[32,24,128]{2,1,0:T(8,128)}, u32[]{:S(2)}) copy-start(f32[32,24,128]{2,1,0:T(8,128)} %param.6) | copy-start | bytes 1179652
  13.6 8.5 %collective-permute-start.2 = (bf16[2,48,128]{2,1,0:T(8,128)(2,1)S(1)}, bf16[2,48,128]{2,1,0:T(8,128)(2,1)S(1)}, u32[]{:S(2)}, u32[]{:S(2)}) collective-permute-start(bf16[2,48,128]{2,1,0:T(8,128)(2,1)S(1)} %get-tuple-element.20), channel_id=1, source_target_pairs={{1,2},{2,1},{3,4},{4,3},{5,6},{6,5},{7,8},{8,7},{9,10},{10,9},{11,... | collective-permute-start | bytes 73736 | tf_op jit(solution)/shard_map/ppermute | solution.py:27
  14.4 7.7 %collective-permute-start.3 = (bf16[2,48,128]{2,1,0:T(8,128)(2,1)S(1)}, bf16[2,48,128]{2,1,0:T(8,128)(2,1)S(1)}, u32[]{:S(2)}, u32[]{:S(2)}) collective-permute-start(bf16[2,48,128]{2,1,0:T(8,128)(2,1)S(1)} %get-tuple-element.21), channel_id=1, source_target_pairs={{0,1},{1,0},{2,3},{3,2},{4,5},{5,4},{6,7},{7,6},{8,9},{9,8},{10,11... | collective-permute-start | bytes 73736 | tf_op jit(solution)/shard_map/ppermute | solution.py:27
  24.0 18.8 %all-to-all-start = ((bf16[16,2,24,128]{3,2,1,0:T(8,128)(2,1)}), bf16[16,2,24,128]{3,2,1,0:T(8,128)(2,1)S(1)}, u32[]{:S(2)}, u32[]{:S(2)}) async-start(bf16[16,2,24,128]{3,2,1,0:T(8,128)(2,1)} %get-tuple-element.30), calls=%async_computation | async-start | bytes 393216 | tf_op jit(solution)/shard_map/all_to_all | solution.py:259
  43.0 10.8 %collective-permute-start.4 = (bf16[2,24,128]{2,1,0:T(8,128)(2,1)S(1)}, bf16[2,24,128]{2,1,0:T(8,128)(2,1)S(1)}, u32[]{:S(2)}, u32[]{:S(2)}) collective-permute-start(bf16[2,24,128]{2,1,0:T(8,128)(2,1)S(1)} %get-tuple-element.32), channel_id=1, source_target_pairs={{0,256},{16,272},{32,288},{48,304},{64,320},{80,336},{96,352},{112... | collective-permute-start | bytes 36872 | tf_op jit(solution)/shard_map/ppermute | solution.py:274

commit v6 on v5

--- a/solution.py
+++ b/solution.py
@@ -210,8 +210,11 @@
         return all_inside_ref[k - 2].astype(jnp.bfloat16)
 
     fill_windows(windows, first_ref, second_ref, inside, width)
-    my_outer[...] = in_outer[...]
-    my_inner[...] = in_inner[...]
+    for n in range(steps):
+        for start in (0, width - 8):
+            rows = pl.ds(n * width + start, 8)
+            my_outer[rows, :] = in_outer[rows, :]
+            my_inner[rows, :] = in_inner[rows, :]
     my_next[...] = in_next[...]
     coupled = [
         coupled_pair(e * (width - 2), 2, windows.at[e], couple, blocks_ref) for e in range(2)
@@ -225,8 +228,11 @@
     y = jnp.zeros((width, 128), jnp.float32)
     for n in range(steps):
         rows = pl.ds(n * width, width)
-        z = 0.5 * (my_inner[rows, :] + z)
-        y = 0.5 * (my_outer[rows, :] + z + y)
+        low, middle, high = pl.ds(n * width, 8), pl.ds(n * width + 8, width - 16), pl.ds((n + 1) * width - 8, 8)
+        inner = jnp.concatenate([my_inner[low, :], in_inner[middle, :], my_inner[high, :]], 0)
+        outer = jnp.concatenate([my_outer[low, :], in_outer[middle, :], my_outer[high, :]], 0)
+        z = 0.5 * (inner + z)
+        y = 0.5 * (outer + z + y)
         result_ref[rows, :] = state_ref[rows, :] + relaxation * y
     ends_outer = (y + my_next[pl.ds(0, width), :]).astype(jnp.bfloat16)
     ends_inner = (z + my_next[pl.ds(width, width), :]).astype(jnp.bfloat16)

time: 55.9 us -> 55.9 us (level)
  no operation moved by 1% of the time
where the time goes in v6:
time: 55.9 us; the launch traced here: 54.8 us
  starting transfers between devices  33.1 us (59%)
  waiting for transfers between devices  10.8 us (19%)
  Pallas kernels  8.49 us (15%)
  between operations  1.06 us (2%)
  local copies, waits for them, and re-layouts  1.02 us (2%)
    ppermute x2, starting transfers between devices, exchange(): lax.ppermute(second_edge, axis, second)  13.5 us
    all_to_all x1, waiting for transfers between devices, ring_carry(): lax.all_to_all(sent, 'tm', 0, 0, axis_index_groups=members, tiled=True)  9.42 us
    ppermute x1, starting transfers between devices, ring_carry(): other = lax.ppermute(total, 'tm', route)  9.39 us
    all_to_all x1, starting transfers between devices, ring_carry(): lax.all_to_all(sent, 'tm', 0, 0, axis_index_groups=members, tiled=True)  8.63 us
    pallas_call x6, Pallas kernels, run(): pl.pallas_call(kernel, out_shape=results, in_specs=scalar + [vector] * (l...  8.49 us
    ppermute x2, starting transfers between devices, exchange(): lax.ppermute(first_edge, axis, first)  1.59 us
    ppermute x1, waiting for transfers between devices, ring_carry(): other = lax.ppermute(total, 'tm', route)  1.31 us
  transfers between devices with their start and end apart: 6, of which 2 were waited for; matrix products, arithmetic and copies ran while one was open for 0% of the time, Pallas kernels for 9%

profile of v6, /device:TPU:1, one launch (start us, length us, event | category | flops | bytes accessed | tf_op | source)
XLA Modules:
  0.0 54.8 jit_solution(8719906137961418809)
XLA Ops:
  0.0 0.0 copy-start.2
  0.0 1.0 %copy-done.2 = f32[32,24,128]{2,1,0:T(8,128)S(1)} copy-done((f32[32,24,128]{2,1,0:T(8,128)S(1)}, f32[32,24,128]{2,1,0:T(8,128)}, u32[]{:S(2)}) %copy-start.2) | copy-done | bytes 393240
  1.0 0.0 copy-start
  1.0 0.0 copy-start.1
  1.0 0.0 copy-start.4
  1.0 0.0 copy-start.5
  1.0 0.0 copy-start.6
  1.1 0.8 %collective-permute-start = (bf16[2,32,128]{2,1,0:T(8,128)(2,1)S(1)}, bf16[2,32,128]{2,1,0:T(8,128)(2,1)S(1)}, u32[]{:S(2)}, u32[]{:S(2)}) collective-permute-start(bf16[2,32,128]{2,1,0:T(8,128)(2,1)S(1)} %get-tuple-element.18), channel_id=1, source_target_pairs={{1,2},{2,1},{3,4},{4,3},{5,6},{6,5},{7,8},{8,7},{9,10},{10,9},{11,... | collective-permute-start | bytes 49160 | tf_op jit(solution)/shard_map/ppermute | solution.py:27
  1.9 8.3 %collective-permute-start.1 = (bf16[2,32,128]{2,1,0:T(8,128)(2,1)S(1)}, bf16[2,32,128]{2,1,0:T(8,128)(2,1)S(1)}, u32[]{:S(2)}, u32[]{:S(2)}) collective-permute-start(bf16[2,32,128]{2,1,0:T(8,128)(2,1)S(1)} %get-tuple-element.19), channel_id=1, source_target_pairs={{0,1},{1,0},{2,3},{3,2},{4,5},{5,4},{6,7},{7,6},{8,9},{9,8},{10,11... | collective-permute-start | bytes 49160 | tf_op jit(solution)/shard_map/ppermute | solution.py:27
  10.2 0.0 copy-done
  10.2 0.0 copy-done.1
  10.2 0.0 copy-done.4
  10.2 0.0 copy-done.5
  10.2 0.0 copy-done.6
  10.2 2.3 %source_inside.1 = (f32[20,48,128]{2,1,0:T(8,128)S(1)}, f32[20,48,128]{2,1,0:T(8,128)S(1)}) custom-call(s32[5,24]{1,0:T(8,128)S(1)} %bitcast.166, f32[768,128]{1,0:T(8,128)S(1)} %bitcast.161, f32[768,128]{1,0:T(8,128)S(1)} %bitcast.164, f32[24,128]{1,0:T(8,128)S(1)} %copy-done.6, bf16[5,24,128,128]{3,2,1,0:T(8,128)(2,1)S(1)} %copy-done, ...), custom_call_target="tpu_custom_call" | custom-call | flops 188743680 | bytes 4932160 | tf_op jit(solution)/shard_map/source_inside/pallas_call | solution.py:303
  12.5 0.0 collective-permute-done.first_ref
  12.5 0.0 collective-permute-done.1.second_ref
  12.5 1.1 %source_edges.1 = (f32[4,48,128]{2,1,0:T(8,128)S(1)}, f32[4,48,128]{2,1,0:T(8,128)S(1)}, bf16[2,48,128]{2,1,0:T(8,128)(2,1)S(1)}, bf16[2,48,128]{2,1,0:T(8,128)(2,1)S(1)}) custom-call(s32[5,24]{1,0:T(8,128)S(1)} %bitcast.167, bf16[2,32,128]{2,1,0:T(8,128)(2,1)S(1)} %collective-permute-done.first_ref, ...), custom_call_target="tpu_custom_call" | custom-call | flops 37748736 | bytes 1786432 | tf_op jit(solution)/shard_map/source_edges/pallas_call | solution.py:303
  13.6 0.0 copy-start.3
  13.6 0.8 %collective-permute-start.2 = (bf16[2,48,128]{2,1,0:T(8,128)(2,1)S(1)}, bf16[2,48,128]{2,1,0:T(8,128)(2,1)S(1)}, u32[]{:S(2)}, u32[]{:S(2)}) collective-permute-start(bf16[2,48,128]{2,1,0:T(8,128)(2,1)S(1)} %get-tuple-element.20), channel_id=1, source_target_pairs={{1,2},{2,1},{3,4},{4,3},{5,6},{6,5},{7,8},{8,7},{9,10},{10,9},{11,... | collective-permute-start | bytes 73736 | tf_op jit(solution)/shard_map/ppermute | solution.py:27
  14.4 5.3 %collective-permute-start.3 = (bf16[2,48,128]{2,1,0:T(8,128)(2,1)S(1)}, bf16[2,48,128]{2,1,0:T(8,128)(2,1)S(1)}, u32[]{:S(2)}, u32[]{:S(2)}) collective-permute-start(bf16[2,48,128]{2,1,0:T(8,128)(2,1)S(1)} %get-tuple-element.21), channel_id=1, source_target_pairs={{0,1},{1,0},{2,3},{3,2},{4,5},{5,4},{6,7},{7,6},{8,9},{9,8},{10,11... | collective-permute-start | bytes 73736 | tf_op jit(solution)/shard_map/ppermute | solution.py:27
  19.7 2.4 %solve_inside.1 = (f32[768,128]{1,0:T(8,128)S(1)}, f32[768,128]{1,0:T(8,128)S(1)}, f32[48,128]{1,0:T(8,128)S(1)}) custom-call(s32[5,24]{1,0:T(8,128)S(1)} %bitcast.168, f32[20,48,128]{2,1,0:T(8,128)S(1)} %get-tuple-element.22.all_inside_ref, f32[4,48,128]{2,1,0:T(8,128)S(1)} %get-tuple-element.23.all_edges_ref, ...), custom_call_target="tpu_custom_call" | custom-call | flops 283115520 | bytes 4932160 | tf_op jit(solution)/shard_map/solve_inside/pallas_call | solution.py:303
  22.1 0.0 collective-permute-done.2.first_ref
  22.1 0.0 collective-permute-done.3.second_ref
  22.1 0.0 copy-done.3
  22.1 1.9 %solve_edges.1 = (f32[768,128]{1,0:T(8,128)S(1)}, bf16[16,2,24,128]{3,2,1,0:T(8,128)(2,1)}) custom-call(s32[5,24]{1,0:T(8,128)S(1)} %bitcast.169, bf16[2,48,128]{2,1,0:T(8,128)(2,1)S(1)} %collective-permute-done.2.first_ref, bf16[2,48,128]{2,1,0:T(8,128)(2,1)S(1)} %collective-permute-done.3.second_ref, f32[20,48,128]{2,1,0:T(8,128)S(1)} %get-tuple-element.22.all_inside_ref, ...), custom_call_target="tpu_custom_call" | custom-call | flops 56623104 | bytes 1786432 | tf_op jit(solution)/shard_map/solve_edges/pallas_call | solution.py:303
  24.0 8.6 %all-to-all-start = ((bf16[16,2,24,128]{3,2,1,0:T(8,128)(2,1)}), bf16[16,2,24,128]{3,2,1,0:T(8,128)(2,1)S(1)}, u32[]{:S(2)}, u32[]{:S(2)}) async-start(bf16[16,2,24,128]{3,2,1,0:T(8,128)(2,1)} %get-tuple-element.30), calls=%async_computation | async-start | bytes 393216 | tf_op jit(solution)/shard_map/all_to_all | solution.py:265
  33.4 9.4 %all-to-all-done = bf16[16,2,24,128]{3,2,1,0:T(8,128)(2,1)S(1)} async-done(((bf16[16,2,24,128]{3,2,1,0:T(8,128)(2,1)}), bf16[16,2,24,128]{3,2,1,0:T(8,128)(2,1)S(1)}, u32[]{:S(2)}, u32[]{:S(2)}) %all-to-all-start) | async-done | bytes 196640 | tf_op jit(solution)/shard_map/all_to_all | solution.py:265
  43.0 9.4 %collective-permute-start.4 = (bf16[2,24,128]{2,1,0:T(8,128)(2,1)S(1)}, bf16[2,24,128]{2,1,0:T(8,128)(2,1)S(1)}, u32[]{:S(2)}, u32[]{:S(2)}) collective-permute-start(bf16[2,24,128]{2,1,0:T(8,128)(2,1)S(1)} %get-tuple-element.32), channel_id=1, source_target_pairs={{0,256},{16,272},{32,288},{48,304},{64,320},{80,336},{96,352},{112... | collective-permute-start | bytes 36872 | tf_op jit(solution)/shard_map/ppermute | solution.py:280
  52.5 1.3 %collective-permute-done.4 = bf16[2,24,128]{2,1,0:T(8,128)(2,1)S(1)} collective-permute-done((bf16[2,24,128]{2,1,0:T(8,128)(2,1)S(1)}, bf16[2,24,128]{2,1,0:T(8,128)(2,1)S(1)}, u32[]{:S(2)}, u32[]{:S(2)}) %collective-permute-start.4) | collective-permute-done | bytes 12320 | tf_op jit(solution)/shard_map/ppermute | solution.py:280
  53.9 0.1 fusion.15.carry_ref
  54.0 0.8 %finish_kernel.1 = f32[768,128]{1,0:T(8,128)} custom-call(f32[768,128]{1,0:T(8,128)S(1)} %get-tuple-element.29.local_ref, f32[2,24,128]{2,1,0:T(8,128)S(1)} %fusion.15.carry_ref), custom_call_target="tpu_custom_call" | custom-call | flops 1572864 | bytes 1196608 | tf_op jit(solution)/shard_map/finish_kernel/pallas_call | solution.py:303
  (17 shorter events, 0.3 us)
Async XLA Ops:
  0.0 1.0 %copy-start.2 = (f32[32,24,128]{2,1,0:T(8,128)S(1)}, f32[32,24,128]{2,1,0:T(8,128)}, u32[]{:S(2)}) copy-start(f32[32,24,128]{2,1,0:T(8,128)} %param.6) | copy-start | bytes 1179652
  1.0 9.2 %copy-start = (bf16[5,24,128,128]{3,2,1,0:T(8,128)(2,1)S(1)}, bf16[5,24,128,128]{3,2,1,0:T(8,128)(2,1)}, u32[]{:S(2)}) copy-start(bf16[5,24,128,128]{3,2,1,0:T(8,128)(2,1)} %blocks_ref.7) | copy-start | bytes 11796484
  1.0 9.2 %copy-start.1 = (bf16[24,128,128]{2,1,0:T(8,128)(2,1)S(1)}, bf16[24,128,128]{2,1,0:T(8,128)(2,1)}, u32[]{:S(2)}) copy-start(bf16[24,128,128]{2,1,0:T(8,128)(2,1)} %precond_ref.7) | copy-start | bytes 2359300
  1.0 9.2 %copy-start.4 = (f32[32,24,128]{2,1,0:T(8,128)S(1)}, f32[32,24,128]{2,1,0:T(8,128)}, u32[]{:S(2)}) copy-start(f32[32,24,128]{2,1,0:T(8,128)} %param.7) | copy-start | bytes 1179652
  1.0 9.2 %copy-start.5 = (s32[24,5]{0,1:T(8,128)S(1)}, s32[24,5]{0,1:T(8,128)}, u32[]{:S(2)}) copy-start(s32[24,5]{0,1:T(8,128)} %param.11) | copy-start | bytes 1444
  1.0 9.2 %copy-start.6 = (f32[24,128]{1,0:T(8,128)S(1)}, f32[24,128]{1,0:T(8,128)}, u32[]{:S(2)}) copy-start(f32[24,128]{1,0:T(8,128)} %initial_ref.3) | copy-start | bytes 36868
  1.1 11.4 %collective-permute-start = (bf16[2,32,128]{2,1,0:T(8,128)(2,1)S(1)}, bf16[2,32,128]{2,1,0:T(8,128)(2,1)S(1)}, u32[]{:S(2)}, u32[]{:S(2)}) collective-permute-start(bf16[2,32,128]{2,1,0:T(8,128)(2,1)S(1)} %get-tuple-element.18), channel_id=1, source_target_pairs={{1,2},{2,1},{3,4},{4,3},{5,6},{6,5},{7,8},{8,7},{9,10},{10,9},{11,... | collective-permute-start | bytes 49160 | tf_op jit(solution)/shard_map/ppermute | solution.py:27
  1.9 10.6 %collective-permute-start.1 = (bf16[2,32,128]{2,1,0:T(8,128)(2,1)S(1)}, bf16[2,32,128]{2,1,0:T(8,128)(2,1)S(1)}, u32[]{:S(2)}, u32[]{:S(2)}) collective-permute-start(bf16[2,32,128]{2,1,0:T(8,128)(2,1)S(1)} %get-tuple-element.19), channel_id=1, source_target_pairs={{0,1},{1,0},{2,3},{3,2},{4,5},{5,4},{6,7},{7,6},{8,9},{9,8},{10,11... | collective-permute-start | bytes 49160 | tf_op jit(solution)/shard_map/ppermute | solution.py:27
  13.6 8.6 %copy-start.3 = (f32[32,24,128]{2,1,0:T(8,128)S(1)}, f32[32,24,128]{2,1,0:T(8,128)}, u32[]{:S(2)}) copy-start(f32[32,24,128]{2,1,0:T(8,128)} %param.6) | copy-start | bytes 1179652
  13.6 8.5 %collective-permute-start.2 = (bf16[2,48,128]{2,1,0:T(8,128)(2,1)S(1)}, bf16[2,48,128]{2,1,0:T(8,128)(2,1)S(1)}, u32[]{:S(2)}, u32[]{:S(2)}) collective-permute-start(bf16[2,48,128]{2,1,0:T(8,128)(2,1)S(1)} %get-tuple-element.20), channel_id=1, source_target_pairs={{1,2},{2,1},{3,4},{4,3},{5,6},{6,5},{7,8},{8,7},{9,10},{10,9},{11,... | collective-permute-start | bytes 73736 | tf_op jit(solution)/shard_map/ppermute | solution.py:27
  14.4 7.7 %collective-permute-start.3 = (bf16[2,48,128]{2,1,0:T(8,128)(2,1)S(1)}, bf16[2,48,128]{2,1,0:T(8,128)(2,1)S(1)}, u32[]{:S(2)}, u32[]{:S(2)}) collective-permute-start(bf16[2,48,128]{2,1,0:T(8,128)(2,1)S(1)} %get-tuple-element.21), channel_id=1, source_target_pairs={{0,1},{1,0},{2,3},{3,2},{4,5},{5,4},{6,7},{7,6},{8,9},{9,8},{10,11... | collective-permute-start | bytes 73736 | tf_op jit(solution)/shard_map/ppermute | solution.py:27
  24.0 18.8 %all-to-all-start = ((bf16[16,2,24,128]{3,2,1,0:T(8,128)(2,1)}), bf16[16,2,24,128]{3,2,1,0:T(8,128)(2,1)S(1)}, u32[]{:S(2)}, u32[]{:S(2)}) async-start(bf16[16,2,24,128]{3,2,1,0:T(8,128)(2,1)} %get-tuple-element.30), calls=%async_computation | async-start | bytes 393216 | tf_op jit(solution)/shard_map/all_to_all | solution.py:265
  43.0 10.8 %collective-permute-start.4 = (bf16[2,24,128]{2,1,0:T(8,128)(2,1)S(1)}, bf16[2,24,128]{2,1,0:T(8,128)(2,1)S(1)}, u32[]{:S(2)}, u32[]{:S(2)}) collective-permute-start(bf16[2,24,128]{2,1,0:T(8,128)(2,1)S(1)} %get-tuple-element.32), channel_id=1, source_target_pairs={{0,256},{16,272},{32,288},{48,304},{64,320},{80,336},{96,352},{112... | collective-permute-start | bytes 36872 | tf_op jit(solution)/shard_map/ppermute | solution.py:280
